TPU v7x, 256 devices: a whole 4x4x8 slice. The times are simulated.
256 devices in a mesh: row: 16 (over z, x_hi), col: 16 (over y, x_lo, core).
Axes of the slice: x: 4 (x_hi: 2, x_lo: 2; x = x_hi * 2 + x_lo), y: 4, z: 8, core: 2. Of those that a mesh axis runs over, the one named last changes fastest.
Arguments:
- front_base: float32 [8, 16, 128, 8, 16, 128], P(None, 'row', None, None, 'col')
- traces: bfloat16 [8, 16, 4, 3, 128, 128], P(None, 'row'), may hold values from -0.75 to 0.75
- adjacency: int32 [128, 4], replicated, may hold values from 0 to 127, as said below
- pivot_order: int32 [2, 512], replicated, may hold values from 0 to 511, each once within a row
- pivot_kind: int32 [2, 512], replicated, may hold values from 0 to 2, as said below
- inverse_diagonal: float32 [2, 512], replicated, may hold values from -0.3 to 0.3
- inverse_coupling: float32 [2, 512], replicated, may hold values from -0.3 to 0.3
- readers: int32 [2, 128], replicated, may hold values 0 or 1
Outputs:
- trailing: float32 [8, 16, 128, 8, 16, 128], P(None, 'row', None, None, 'col')
Inputs may be any that keep to these rules, and one draw needn't show every extreme that they name: The elements form a 16 x 8 grid that closes on itself in both dimensions, numbered in a drawn order; faces 0 and 1 lead to the next and previous element along the first dimension, 2 and 3 along the second, so adjacency[adjacency[e, f], f with its lowest bit flipped] = e. `pivot_kind`: 0 marks a 1 x 1 pivot; 1 marks the first position of a 2 x 2 pivot, whose second position follows and is marked 2; 2 x 2 pivots start at even positions.
All inputs are finite; a program needn't handle non-finite values.
Results may differ from a plain program's by a relative error of at most 0.008.
Values may be sent and summed in bfloat16 or wider, within the bound.
No kernel may reach another device: no remote copies, remote signals or barrier semaphores. Data moves between devices by JAX's collectives and lax.ppermute only.
A program may use at most 128 MiB of HBM per device.

v0:
```python
import jax
import jax.numpy as jnp
from jax import lax
from jax.sharding import PartitionSpec as P

NB = 128
PW = 512
PANELS = 2


def from_root(array, axis, root):
    mine = lax.axis_index(axis) == root
    return lax.psum(jnp.where(mine, array, jnp.zeros_like(array)), axis)


def face_left(values):
    return jnp.concatenate(
        [values[:, :, 0], values[:, :, 0], values[:, :, 1], values[:, :, 2]], axis=2
    )


def face_right(values):
    return jnp.concatenate(
        [
            4.0 * values[:, :, 0],
            -0.5 * values[:, :, 1],
            -0.5 * values[:, :, 0],
            2.0 * values[:, :, 2],
        ],
        axis=2,
    )


def apply_inverse(values, pivot_kinds, diagonal, pair_terms):
    starts = (pivot_kinds == 1).astype(values.dtype)
    upward = pair_terms * starts
    upward_prev = jnp.concatenate([jnp.zeros_like(upward[:1]), upward[:-1]])
    following = jnp.concatenate([values[:, 1:], jnp.zeros_like(values[:, :1])], axis=1)
    preceding = jnp.concatenate([jnp.zeros_like(values[:, :1]), values[:, :-1]], axis=1)
    return values * diagonal + following * upward + preceding * upward_prev


def local(
    front_base,
    traces,
    adjacency,
    pivot_order,
    pivot_kind,
    inverse_diagonal,
    inverse_coupling,
    readers,
):
    row_count = lax.axis_size("row")
    col_count = lax.axis_size("col")
    row_index = lax.axis_index("row")
    col_index = lax.axis_index("col")
    row_blocks = front_base.shape[0]
    col_blocks = front_base.shape[3]
    rows_total = row_blocks * NB
    local_traces = traces[:, 0]
    copy_index = 0
    received = [from_root(local_traces, "row", col_index + copy_index * col_count)]
    column_traces = jnp.stack(received, axis=1).reshape((col_blocks,) + local_traces.shape[1:])
    left_parts = face_left(local_traces)
    right_parts = face_right(local_traces)
    column_right = face_right(column_traces)
    opposite = jnp.array([1, 0, 3, 2], dtype=jnp.int32)
    local_elements = jnp.arange(row_blocks, dtype=jnp.int32) * row_count + row_index
    neighbour = jnp.take(adjacency, local_elements, axis=0)
    held_here = neighbour % col_count == col_index
    col_slot = neighbour // col_count
    partner = column_right[col_slot, opposite[None, :]]
    coupling = jnp.einsum(
        "efqi,efqj->efij", left_parts, partner, preferred_element_type=jnp.float32
    )
    self_terms = jnp.einsum(
        "efqi,efqj->eij", left_parts, right_parts, preferred_element_type=jnp.float32
    )
    slot_ids = jnp.arange(col_blocks, dtype=jnp.int32)
    place_pair = (held_here[:, :, None] & (col_slot[:, :, None] == slot_ids[None, None, :])).astype(
        jnp.float32
    )
    self_here = (local_elements % col_count == col_index)[:, None]
    place_self = (self_here & ((local_elements // col_count)[:, None] == slot_ids[None, :])).astype(
        jnp.float32
    )
    assembled = jnp.einsum("eij,ec->eicj", self_terms, place_self, precision=lax.Precision.HIGHEST)
    assembled = assembled - jnp.einsum(
        "efij,efc->eicj", coupling, place_pair, precision=lax.Precision.HIGHEST
    )
    front_mat = front_base.reshape(rows_total, col_blocks * NB) + assembled.reshape(
        rows_total, col_blocks * NB
    )
    panel_blocks = PW // NB
    for which_panel in range(PANELS):
        first_block = which_panel * panel_blocks
        front_slots = front_mat.reshape(rows_total, col_blocks, NB)
        low_slot = first_block // col_count
        high_slot = (first_block + panel_blocks - 1) // col_count
        slab_cols = front_slots[:, low_slot : high_slot + 1, :].astype(jnp.bfloat16)[:, :, None, :]
        gathered = lax.all_gather(slab_cols, "col", axis=2, tiled=True)
        gathered = gathered.reshape(rows_total, -1, NB)
        begin_block = first_block - low_slot * col_count
        columns = gathered[:, begin_block : begin_block + panel_blocks, :].reshape(rows_total, PW)
        columns = jnp.take(columns, pivot_order[which_panel], axis=1)
        kept_blocks = jnp.take(readers[which_panel], local_elements) * (
            local_elements >= first_block + panel_blocks
        ).astype(jnp.int32)
        kept_rows = jnp.repeat(kept_blocks, NB).astype(jnp.bfloat16)
        panel_vals = columns * kept_rows[:, None]
        scaled = apply_inverse(
            panel_vals.astype(jnp.float32),
            pivot_kind[which_panel],
            inverse_diagonal[which_panel],
            inverse_coupling[which_panel],
        ).astype(jnp.bfloat16)
        copy_index = 0
        incoming = from_root(panel_vals, "row", col_index + copy_index * col_count)
        transposed = [incoming.reshape(row_blocks, NB, PW)]
        col_panel = jnp.stack(transposed, axis=1).reshape(col_blocks * NB, PW)
        front_mat = front_mat - lax.dot_general(
            scaled, col_panel, (((1,), (1,)), ((), ())), preferred_element_type=jnp.float32
        )
    return front_mat.reshape(row_blocks, 1, NB, col_blocks, 1, NB)


def solution(mesh):
    in_specs = (
        P(None, "row", None, None, "col", None),
        P(None, "row", None, None, None, None),
        P(),
        P(),
        P(),
        P(),
        P(),
        P(),
    )
    out_specs = P(None, "row", None, None, "col", None)
    return jax.shard_map(local, mesh=mesh, in_specs=in_specs, out_specs=out_specs, check_vma=False)
```

profile of v0, /device:TPU:8, one launch (start us, length us, event | category | flops | bytes accessed | tf_op | source)
XLA Modules:
  0.0 654.4 jit_solution(11187019615183884576)
XLA Ops:
  6.5 3.8 broadcast_select_fusion
  10.4 2.1 copy.69
  13.5 5.0 copy.39
  20.8 2.8 fusion.10
  23.6 169.1 %all-reduce.8.cloned.1.call-done = bf16[8,4,3,128,128]{4,3,1,0,2:T(8,128)(2,1)} async-done(((bf16[8,4,3,128,128]{4,3,1,0,2:T(8,128)(2,1)}), bf16[8,4,3,128,128]{4,3,1,0,2:T(8,128)(2,1)}) %all-reduce.8.cloned.1.call-update) | async-done | bytes 3145744 | tf_op jit(solution)/shard_map/psum | solution.py:13
  192.7 2.2 multiply_bitcast_fusion.1
  194.9 2.2 pad_maximum_fusion.1
  197.1 5.4 gather_fusion.1
  202.6 3.2 fusion.9
  205.8 4.5 multiply_subtract_fusion
  210.4 2.0 copy-done
  212.6 1.8 fusion.21
  215.4 36.0 %all-gather.5.cloned.1.call-done = bf16[1024,16,128]{2,0,1:T(8,128)(2,1)} async-done(((bf16[1024,1,128]{2,0,1:T(8,128)(2,1)}), bf16[1024,16,128]{2,0,1:T(8,128)(2,1)}) %all-gather.5.cloned.1.call-update) | async-done | bytes 4194320 | tf_op jit(solution)/shard_map/all_gather | solution.py:101
  251.4 1.3 slice.140
  253.2 2.1 gather_fusion.2
  255.3 1.3 fusion.47
  256.8 5.2 copy.68
  262.0 5.4 copy.51
  267.5 5.3 copy.67
  272.8 5.5 copy.38
  278.2 2.4 fusion.50
  280.6 137.7 %all-reduce.10.cloned.1.call-done = bf16[1024,512]{0,1:T(8,128)(2,1)} async-done(((bf16[1024,512]{0,1:T(8,128)(2,1)}), bf16[1024,512]{0,1:T(8,128)(2,1)}) %all-reduce.10.cloned.1.call-update) | async-done | bytes 1048592 | tf_op jit(solution)/shard_map/psum | solution.py:13
  418.4 8.7 %fusion.53 = (bf16[1024,1024]{0,1:T(8,128)(2,1)S(1)}, f32[1024,1024]{0,1:T(8,128)}) fusion(bf16[1024,512]{0,1:T(8,128)(2,1)} %all-reduce.10.cloned.1.call-done, f32[1024,511]{0,1:T(8,128)} %get-tuple-element.21, f32[1024,511]{0,1:T(8,128)} %get-tuple-element.20, f32[512]{0:T(512)S(1)} %pad_maximum_fusion.7, f32[512]{0:T(512)S(1)} %bitcast.126, ...), kind=kOutput, calls=%fused_computation.126 | convolution fusion | flops 1081606144 | bytes 20972032 | tf_op jit(solution)/shard_map/dot_general | solution.py:121
  428.8 36.9 %all-gather.7.cloned.1.call-done = bf16[1024,16,128]{2,0,1:T(8,128)(2,1)} async-done(((bf16[1024,1,128]{2,0,1:T(8,128)(2,1)}), bf16[1024,16,128]{2,0,1:T(8,128)(2,1)}) %all-gather.7.cloned.1.call-update) | async-done | bytes 4194320 | tf_op jit(solution)/shard_map/all_gather | solution.py:101
  465.7 1.3 slice.145
  467.5 2.1 gather_fusion.4
  469.6 1.3 fusion.48
  471.0 2.3 fusion.49
  473.3 159.0 %all-reduce.12.cloned.1.call-done = bf16[1024,512]{0,1:T(8,128)(2,1)} async-done(((bf16[1024,512]{0,1:T(8,128)(2,1)}), bf16[1024,512]{0,1:T(8,128)(2,1)}) %all-reduce.12.cloned.1.call-update) | async-done | bytes 1048592 | tf_op jit(solution)/shard_map/psum | solution.py:13
  632.3 5.5 subtract_bitcast_fusion
  637.7 3.0 copy.56
  640.7 7.2 %copy.45 = f32[8,1,128,8,1,128]{5,4,3,2,1,0:T(1,128)} copy(f32[8,1,128,8,1,128]{2,0,5,3,4,1:T(8,128)} %bitcast.118) | data formatting | bytes 8388608 | tf_op jit(solution)/shard_map/reshape | solution.py:124
  (78 shorter events, 7.6 us)
Async XLA Ops:
  6.5 186.2 %all-reduce.8.cloned.1.call-start = ((), (), s32[]{:S(2)}) async-start(), calls=%async_computation | async-start | bytes 6291456 | tf_op jit(solution)/shard_map/psum | solution.py:13
  10.3 2.2 copy-start.12
  10.3 3.0 copy-start.14
  10.3 241.0 %all-gather.5.cloned.1.call-start = ((), (), s32[]{:S(2)}) async-start(), calls=%async_computation.3 | async-start | bytes 4456448 | tf_op jit(solution)/shard_map/all_gather | solution.py:101
  19.1 1.0 copy-start.1
  19.2 1.3 copy-start.3
  19.2 1.7 copy-start.5
  197.1 5.4 copy-start.2
  197.1 5.4 copy-start.4
  197.1 5.4 copy-start.6
  202.6 3.2 copy-start.7
  205.8 8.8 %copy-start.13 = (s32[2,128]{1,0:T(2,128)S(1)}, s32[2,128]{1,0:T(2,128)}, u32[]{:S(2)}) copy-start(s32[2,128]{1,0:T(2,128)} %param.20) | copy-start | bytes 3076
  205.8 9.4 %copy-start.10 = (s32[2,512]{1,0:T(2,128)S(1)}, s32[2,512]{1,0:T(2,128)}, u32[]{:S(2)}) copy-start(s32[2,512]{1,0:T(2,128)} %param.16) | copy-start | bytes 12292
  210.4 2.0 copy-start
  214.5 203.9 %all-reduce.10.cloned.1.call-start = ((), (), s32[]{:S(2)}) async-start(), calls=%async_computation.1 | async-start | bytes 2097152 | tf_op jit(solution)/shard_map/psum | solution.py:13
  256.6 209.1 %all-gather.7.cloned.1.call-start = ((), (), s32[]{:S(2)}) async-start(), calls=%async_computation.4 | async-start | bytes 4456448 | tf_op jit(solution)/shard_map/all_gather | solution.py:101
  262.0 5.4 copy-start.8
  262.0 5.4 copy-start.9
  262.0 5.5 copy-start.11
  428.0 204.3 %all-reduce.12.cloned.1.call-start = ((), (), s32[]{:S(2)}) async-start(), calls=%async_computation.2 | async-start | bytes 2097152 | tf_op jit(solution)/shard_map/psum | solution.py:13
Sparse Core Ops, SparseCore 0:
  10.4 182.2 all-reduce.7
  214.6 36.6 all-gather.4
  256.7 161.6 all-reduce.9
  428.1 37.5 all-gather.6
  471.0 161.2 all-reduce.11
where the time goes:
time: 655 us; the launch traced here: 654 us
  waiting for transfers between devices  539 us (82%)
  local copies, waits for them, and re-layouts  63.8 us (10%)
  matrix products  24.7 us (4%)
  other arithmetic  13.4 us (2%)
  between operations  13.4 us (2%)
    psum x3, waiting for transfers between devices, from_root(): return lax.psum(jnp.where(mine, array, jnp.zeros_like(array)), axis)  466 us
    all_gather x2, waiting for transfers between devices, local(): gathered = lax.all_gather(slab_cols, 'col', axis=2, tiled=True)  72.9 us
    unnamed x37, local copies, waits for them, and re-layouts  24.8 us
    dot_general x2, matrix products, local(): lax.dot_general(scaled, col_panel, (((1,), (1,)), ((), ())), preferred_el...  14.2 us
  transfers between devices with their start and end apart: 5, of which 5 were waited for; matrix products, arithmetic and copies ran while one was open for 6% of the time, Pallas kernels for 0%

commit v1 on v0

v1 whole, which is shorter than its diff:
```python
import jax
import jax.numpy as jnp
from jax import lax
from jax.experimental import pallas as pl
from jax.experimental.pallas import tpu as pltpu
from jax.sharding import PartitionSpec as P

NB = 128
PW = 512
N = 16
BOTH = ("row", "col")
F32 = jnp.float32
BF16 = jnp.bfloat16

SWAP_X = [(r, r ^ 1) for r in range(N)]
Z_LINES = [[2 * z + x for z in range(8)] for x in (0, 1)]


def spread_target(q, j):
    return 2 * ((q // 2 + j // 2) % 8) + j % 2


SPREAD = [(q * N + j, spread_target(q, j) * N + q) for q in range(N) for j in range(N)]
SPREAD_LOW = [(s, d) for s, d in SPREAD if s // N < 8]
HALVE = [(n, n + 8) for n in range(8)]


def left_of(ref, lead):
    v, s, l = ref[lead + (0,)], ref[lead + (1,)], ref[lead + (2,)]
    return jnp.concatenate([v, v, s, l], axis=0)


def right_of(ref, lead):
    v, s, l = ref[lead + (0,)], ref[lead + (1,)], ref[lead + (2,)]
    return jnp.concatenate([v * 4.0, s * -0.5, v * -0.5, l * 2.0], axis=0).astype(BF16)


def pair_product(left, right):
    return lax.dot_general(left, right, (((0,), (0,)), ((), ())), preferred_element_type=F32)


def panel_block_kernel(place, adj, base, own, faces, out, acc):
    r, c = place[0], place[1]
    acc[...] = base[...]
    for g in range(4):
        e = adj[c * 4 + g]

        @pl.when((e % N == r) & (c < 8))
        def _():
            a = e // N
            acc[a] -= pair_product(left_of(own, (a, g ^ 1)), right_of(faces, (g,)))

    @pl.when(r == c)
    def _():
        for f in range(4):
            acc[0] += pair_product(left_of(own, (0, f)), right_of(own, (0, f)))

    out[...] = acc[...].astype(BF16)


def assemble_kernel(place, adj, base, own, faces, out):
    r, c = place[0], place[1]
    a = pl.program_id(0)
    out[...] = base[...]
    for f in range(4):
        n = adj[(a * N + r) * 4 + f]

        @pl.when(n % N == c)
        def _():
            g = f ^ 1
            b = n // N
            right = right_of(faces, (b, (g // 2) ^ (r % 2), g % 2))
            rows = pl.ds(b, NB, stride=8)
            out[0, rows, :] = out[0, rows, :] - pair_product(left_of(own, (0, f)), right)

    @pl.when(r == c)
    def _():
        total = pair_product(left_of(own, (0, 0)), right_of(own, (0, 0)))
        for f in range(1, 4):
            total += pair_product(left_of(own, (0, f)), right_of(own, (0, f)))
        rows = pl.ds(a, NB, stride=8)
        out[0, rows, :] = out[0, rows, :] + total


def dot_nt(x, y):
    return lax.dot_general(x, y, (((1,), (1,)), ((), ())), preferred_element_type=F32)


def scale(values, partner, diag, side):
    swapped = jnp.dot(values, partner, preferred_element_type=F32)
    return (values.astype(F32) * diag + swapped * side).astype(BF16)


def keep(readers, k, e):
    return jnp.where((readers[k * 128 + e] == 1) & (e >= 4 * (k + 1)), 1.0, 0.0).astype(F32)


def update_kernel(
    place, readers, front, row_half, col_half, cross, partner, diag, side, out,
    v0c, v1c, cross_t, v0r, f1r,
):
    r, c = place[0], place[1]
    step = pl.program_id(0)

    @pl.when(step == 0)
    def _():
        for i in range(4):
            kept = keep(readers, 0, 4 + i)
            for n in range(4):
                for s in range(4):
                    tile = cross[4 * n + s, i].astype(F32) * kept
                    cross_t[i * NB + s * 32 : i * NB + (s + 1) * 32, n * NB : (n + 1) * NB] = tile.astype(BF16)
        for b in range(8):
            e = b * N + c
            kept = keep(readers, 0, e)
            for n in range(8):
                j = n + 8 * (b // 4)
                tile = col_half[(j // 2 + c // 2) % 8, (j % 2) ^ (r % 2), b % 4]
                rows = slice(b * NB, (b + 1) * NB)
                if n < 4:
                    v0c[rows, n * NB : (n + 1) * NB] = (tile.astype(F32) * kept).astype(BF16)
                else:
                    v1c[rows, (n - 4) * NB : (n - 3) * NB] = tile
        w0c = scale(v0c[...], partner[0], diag[0:1], side[0:1])
        fresh = v1c[...].astype(F32) - dot_nt(w0c, cross_t[...])
        for b in range(8):
            kept = keep(readers, 1, b * N + c)
            v1c[b * NB : (b + 1) * NB, :] = (fresh[b * NB : (b + 1) * NB] * kept).astype(BF16)

    for t in range(2):
        a = 2 * step + t
        kept = keep(readers, 0, a * N + r)
        rows = slice(t * NB, (t + 1) * NB)
        for n in range(8):
            tile = row_half[n + 8 * (a // 4), a % 4]
            if n < 4:
                v0r[rows, n * NB : (n + 1) * NB] = (tile.astype(F32) * kept).astype(BF16)
            else:
                f1r[rows, (n - 4) * NB : (n - 3) * NB] = tile
    w0r = scale(v0r[...], partner[0], diag[0:1], side[0:1])
    fresh = f1r[...].astype(F32) - dot_nt(w0r, cross_t[...])
    for t in range(2):
        kept = keep(readers, 1, (2 * step + t) * N + r)
        f1r[t * NB : (t + 1) * NB, :] = (fresh[t * NB : (t + 1) * NB] * kept).astype(BF16)
    w1r = scale(f1r[...], partner[1], diag[1:2], side[1:2])
    change = dot_nt(w0r, v0c[...]) + dot_nt(w1r, v1c[...])
    for t in range(2):
        for b in range(8):
            rows = pl.ds(b, NB, stride=8)
            out[t, rows, :] = front[t, rows, :] - change[t * NB : (t + 1) * NB, b * NB : (b + 1) * NB]


def pivot_tables(pivot_order, pivot_kind, inverse_diagonal, inverse_coupling):
    at = pivot_order[:, :, None] == jnp.arange(PW, dtype=jnp.int32)[None, None, :]
    starts = jnp.where(pivot_kind == 1, inverse_coupling, 0.0).reshape(2, PW // 2, 2)[:, :, 0]
    factor = jnp.repeat(starts, 2, axis=1)
    diag = jnp.sum(jnp.where(at, inverse_diagonal[:, :, None], 0.0), axis=1)
    side = jnp.sum(jnp.where(at, factor[:, :, None], 0.0), axis=1)
    order_swapped = pivot_order.reshape(2, PW // 2, 2)[:, :, ::-1].reshape(2, PW)
    partner_of = jnp.sum(jnp.where(at, order_swapped[:, :, None], 0), axis=1)
    partner = (jnp.arange(PW, dtype=jnp.int32)[None, :, None] == partner_of[:, None, :]).astype(BF16)
    return partner, diag, side


def smem():
    return pl.BlockSpec(memory_space=pltpu.SMEM)


def vmem():
    return pl.BlockSpec(memory_space=pltpu.VMEM)


def local(
    front_base, traces, adjacency, pivot_order, pivot_kind, inverse_diagonal, inverse_coupling, readers,
):
    r = lax.axis_index("row")
    c = lax.axis_index("col")
    place = jnp.stack([r, c]).astype(jnp.int32)
    adj = adjacency.reshape(-1)
    own = traces[:, 0]
    base = front_base.reshape(8, 8 * NB, NB)

    low_faces = lax.ppermute(own[0], BOTH, SPREAD_LOW)

    target = 2 * ((r // 2 + c // 2) % 8) + c % 2
    piece = lax.dynamic_slice_in_dim(own.reshape(32, 3, NB, NB), 2 * target, 2, axis=0)
    piece = lax.ppermute(piece, BOTH, SPREAD)
    both = jnp.stack([piece, lax.ppermute(piece, "row", SWAP_X)])
    faces = lax.all_gather(both, "row", axis=0, axis_index_groups=Z_LINES)

    base_low = front_base[:, 0, :, 0, 0, :]
    block = pl.pallas_call(
        panel_block_kernel,
        out_shape=jax.ShapeDtypeStruct((8, NB, NB), BF16),
        in_specs=[smem(), smem(), vmem(), vmem(), vmem()],
        out_specs=vmem(),
        scratch_shapes=[pltpu.VMEM((8, NB, NB), F32)],
        name="panel_block",
    )(place, adj, base_low, own, low_faces)
    upper = lax.ppermute(block[4:], "col", HALVE)
    half = jnp.where(c < 8, block[:4], upper)

    spread = lax.ppermute(half, BOTH, SPREAD)
    pair = jnp.stack([spread, lax.ppermute(spread, "row", SWAP_X)])
    col_half = lax.all_gather(pair, "row", axis=0, axis_index_groups=Z_LINES)

    row_half = lax.all_to_all(jnp.broadcast_to(half[None], (N,) + half.shape), "col", 0, 0, tiled=True)

    first = row_half[:4, 0].reshape(N, 32, NB)
    part = lax.dynamic_index_in_dim(first, c, 0, keepdims=False)
    part = lax.all_to_all(jnp.broadcast_to(part[None], (N, 32, NB)), "row", 0, 0, tiled=True)[4:8]
    cross = lax.all_to_all(jnp.broadcast_to(part[None], (N, 4, 32, NB)), "col", 0, 0, tiled=True)

    partner, diag, side = pivot_tables(pivot_order, pivot_kind, inverse_diagonal, inverse_coupling)

    front = pl.pallas_call(
        assemble_kernel,
        grid=(8,),
        out_shape=jax.ShapeDtypeStruct((8, 8 * NB, NB), F32),
        in_specs=[
            smem(),
            smem(),
            pl.BlockSpec((1, 8 * NB, NB), lambda a: (a, 0, 0)),
            pl.BlockSpec((1, 4, 3, NB, NB), lambda a: (a, 0, 0, 0, 0)),
            vmem(),
        ],
        out_specs=pl.BlockSpec((1, 8 * NB, NB), lambda a: (a, 0, 0)),
        name="assemble",
    )(place, adj, base, own, faces)

    out = pl.pallas_call(
        update_kernel,
        grid=(4,),
        out_shape=jax.ShapeDtypeStruct((8, 8 * NB, NB), F32),
        in_specs=[
            smem(),
            smem(),
            pl.BlockSpec((2, 8 * NB, NB), lambda s: (s, 0, 0)),
            vmem(),
            vmem(),
            vmem(),
            vmem(),
            vmem(),
            vmem(),
        ],
        out_specs=pl.BlockSpec((2, 8 * NB, NB), lambda s: (s, 0, 0)),
        scratch_shapes=[
            pltpu.VMEM((8 * NB, PW), BF16),
            pltpu.VMEM((8 * NB, PW), BF16),
            pltpu.VMEM((PW, PW), BF16),
            pltpu.VMEM((2 * NB, PW), BF16),
            pltpu.VMEM((2 * NB, PW), BF16),
        ],
        name="update",
    )(place, readers.reshape(-1), front, row_half, col_half, cross, partner, diag, side)
    return out.reshape(8, 1, NB, 8, 1, NB)


def solution(mesh):
    in_specs = (
        P(None, "row", None, None, "col", None),
        P(None, "row", None, None, None, None),
        P(),
        P(),
        P(),
        P(),
        P(),
        P(),
    )
    out_specs = P(None, "row", None, None, "col", None)
    return jax.shard_map(local, mesh=mesh, in_specs=in_specs, out_specs=out_specs, check_vma=False)
```

time: 655 us -> 214 us (0.33)
  waiting for transfers between devices: 539 us -> 95.9 us
  starting transfers between devices: 0.35 us -> 61.3 us
  local copies, waits for them, and re-layouts: 63.8 us -> 11.9 us
  matrix products: 24.7 us -> 0 us
  Pallas kernels: 0 us -> 23.2 us
  other arithmetic: 13.4 us -> 6.06 us
    psum x3 -> x0, waiting for transfers between devices: 466 us -> none  [from_root(): return lax.psum(jnp.where(mine, array, jnp.zeros_like(array)), axis)]
    all_gather x2, waiting for transfers between devices: 72.9 us -> 0.02 us  [the longest x1 0.02 us: local(): col_half = lax.all_gather(pair, 'row', axis=0, axis_index_groups=Z_LINES)]
    ppermute x0 -> x6, waiting for transfers between devices: none -> 60.1 us  [the longest x1 29 us: local(): low_faces = lax.ppermute(own[0], BOTH, SPREAD_LOW)]
    all_to_all x0 -> x3, starting transfers between devices: none -> 37.3 us  [the longest x1 24.6 us: local(): lax.all_to_all(jnp.broadcast_to(half[None], (N,) + half.shape), 'col', 0,...]
    all_to_all x0 -> x3, waiting for transfers between devices: none -> 35.8 us  [the longest x1 26.1 us: local(): lax.all_to_all(jnp.broadcast_to(half[None], (N,) + half.shape), 'col', 0,...]
    dot_general x5 -> x0, matrix products: 24.7 us -> none  [the longest x2 14.2 us: local(): lax.dot_general(scaled, col_panel, (((1,), (1,)), ((), ())), preferred_el...]
    ppermute x0 -> x6, starting transfers between devices: none -> 23.9 us  [the longest x1 7.11 us: local(): upper = lax.ppermute(block[4:], 'col', HALVE)]
    pallas_call x0 -> x3, Pallas kernels: none -> 23.2 us  [the longest x1 11.4 us: local(): pl.pallas_call(update_kernel, grid=(4,), out_shape=jax.ShapeDtypeStruct((...]
  transfers between devices with their start and end apart: 5 -> 11, of which waited for: 5 -> 8; matrix products, arithmetic and copies ran while one was open for 6% -> 7% of each run, Pallas kernels for 0% -> 6%
where the time goes in v1:
time: 214 us; the launch traced here: 212 us
  waiting for transfers between devices  95.9 us (45%)
  starting transfers between devices  61.3 us (29%)
  Pallas kernels  23.2 us (11%)
  between operations  13.6 us (6%)
  local copies, waits for them, and re-layouts  11.9 us (6%)
  other arithmetic  6.06 us (3%)
    ppermute x1, waiting for transfers between devices, local(): low_faces = lax.ppermute(own[0], BOTH, SPREAD_LOW)  29 us
    all_to_all x1, waiting for transfers between devices, local(): lax.all_to_all(jnp.broadcast_to(half[None], (N,) + half.shape), 'col', 0,...  26.1 us
    all_to_all x1, starting transfers between devices, local(): lax.all_to_all(jnp.broadcast_to(half[None], (N,) + half.shape), 'col', 0,...  24.6 us
    pallas_call x1, Pallas kernels, local(): pl.pallas_call(update_kernel, grid=(4,), out_shape=jax.ShapeDtypeStruct((...  11.4 us
    ppermute x1, waiting for transfers between devices, local(): spread = lax.ppermute(half, BOTH, SPREAD)  11.3 us
    all_to_all x1, waiting for transfers between devices, local(): lax.all_to_all(jnp.broadcast_to(part[None], (N, 32, NB)), 'row', 0, 0, ti...  9.64 us
    pallas_call x1, Pallas kernels, local(): pl.pallas_call(assemble_kernel, grid=(8,), out_shape=jax.ShapeDtypeStruct...  8.81 us
    all_to_all x1, starting transfers between devices, local(): lax.all_to_all(jnp.broadcast_to(part[None], (N, 32, NB)), 'row', 0, 0, ti...  7.55 us
  transfers between devices with their start and end apart: 11, of which 8 were waited for; matrix products, arithmetic and copies ran while one was open for 7% of the time, Pallas kernels for 6%

profile of v1, /device:TPU:8, one launch (start us, length us, event | category | flops | bytes accessed | tf_op | source)
XLA Modules:
  0.0 212.0 jit_solution(2603561768658962257)
XLA Ops:
  6.5 1.0 constant_dynamic-slice_fusion
  7.5 5.1 %collective-permute-start = (bf16[2,3,128,128]{3,2,1,0:T(8,128)(2,1)S(1)}, bf16[2,3,128,128]{3,2,1,0:T(8,128)(2,1)S(1)}, u32[]{:S(2)}, u32[]{:S(2)}) collective-permute-start(bf16[2,3,128,128]{3,2,1,0:T(8,128)(2,1)S(1)} %constant_dynamic-slice_fusion), channel_id=1, source_target_pairs={{0,0},{1,16},{2,32},{3,48},{4,64},{5,80},{6,96},{7,112},{8,128},{9... | collective-permute-start | bytes 589832 | tf_op jit(solution)/shard_map/ppermute | solution.py:187
  12.6 6.0 %collective-permute-done = bf16[2,3,128,128]{3,2,1,0:T(8,128)(2,1)S(1)} collective-permute-done((bf16[2,3,128,128]{3,2,1,0:T(8,128)(2,1)S(1)}, bf16[2,3,128,128]{3,2,1,0:T(8,128)(2,1)S(1)}, u32[]{:S(2)}, u32[]{:S(2)}) %collective-permute-start) | collective-permute-done | bytes 196640 | tf_op jit(solution)/shard_map/ppermute | solution.py:187
  18.6 6.5 %collective-permute-start.1 = (bf16[2,3,128,128]{3,2,1,0:T(8,128)(2,1)S(1)}, bf16[2,3,128,128]{3,2,1,0:T(8,128)(2,1)S(1)}, u32[]{:S(2)}, u32[]{:S(2)}) collective-permute-start(bf16[2,3,128,128]{3,2,1,0:T(8,128)(2,1)S(1)} %collective-permute-done), channel_id=1, source_target_pairs={{0,16},{16,0},{32,48},{48,32},{64,80},{80,64},{96,112},{112,96},{1... | collective-permute-start | bytes 589832 | tf_op jit(solution)/shard_map/ppermute | solution.py:188
  25.1 3.9 %collective-permute-done.1 = bf16[2,3,128,128]{3,2,1,0:T(8,128)(2,1)S(1)} collective-permute-done((bf16[2,3,128,128]{3,2,1,0:T(8,128)(2,1)S(1)}, bf16[2,3,128,128]{3,2,1,0:T(8,128)(2,1)S(1)}, u32[]{:S(2)}, u32[]{:S(2)}) %collective-permute-start.1) | collective-permute-done | bytes 196640 | tf_op jit(solution)/shard_map/ppermute | solution.py:188
  29.1 0.8 pad_maximum_fusion
  29.9 1.0 slice_bitcast_fusion
  30.9 3.3 %collective-permute-start.2 = (bf16[4,3,128,128]{3,2,1,0:T(8,128)(2,1)S(1)}, bf16[4,3,128,128]{3,2,1,0:T(8,128)(2,1)S(1)}, u32[]{:S(2)}, u32[]{:S(2)}) collective-permute-start(bf16[4,3,128,128]{3,2,1,0:T(8,128)(2,1)S(1)} %slice_bitcast_fusion), channel_id=1, source_target_pairs={{0,0},{1,16},{2,32},{3,48},{4,64},{5,80},{6,96},{7,112},{8,128},{9... | collective-permute-start | bytes 1179656 | tf_op jit(solution)/shard_map/ppermute | solution.py:183
  35.1 1.9 slice.22
  37.6 29.0 %collective-permute-done.2.faces = bf16[4,3,128,128]{3,2,1,0:T(8,128)(2,1)S(1)} collective-permute-done((bf16[4,3,128,128]{3,2,1,0:T(8,128)(2,1)S(1)}, bf16[4,3,128,128]{3,2,1,0:T(8,128)(2,1)S(1)}, u32[]{:S(2)}, u32[]{:S(2)}) %collective-permute-start.2) | collective-permute-done | bytes 393248 | tf_op jit(solution)/shard_map/ppermute | solution.py:183
  66.5 0.8 copy-done.2
  67.3 3.0 %panel_block.1 = bf16[8,128,128]{2,1,0:T(8,128)(2,1)} custom-call(s32[2]{0:T(128)} %pad_add_fusion.place, s32[512]{0:T(512)} %reshape.28.adj, f32[8,128,128]{2,1,0:T(8,128)} %bitcast.29, bf16[8,4,3,128,128]{4,3,2,1,0:T(8,128)(2,1)} %bitcast.24, bf16[4,3,128,128]{3,2,1,0:T(8,128)(2,1)} %copy-done.2), custom_call_target="tpu_custom_call" | custom-call | tf_op jit(solution)/shard_map/panel_block/pallas_call | solution.py:192
  70.3 0.9 slice.30
  71.2 7.1 %collective-permute-start.3 = (bf16[4,128,128]{2,1,0:T(8,128)(2,1)S(1)}, bf16[4,128,128]{2,1,0:T(8,128)(2,1)S(1)}, u32[]{:S(2)}, u32[]{:S(2)}) collective-permute-start(bf16[4,128,128]{2,1,0:T(8,128)(2,1)S(1)} %slice.30), channel_id=1, source_target_pairs={{0,8},{1,9},{2,10},{3,11},{4,12},{5,13},{6,14},{7,15},{16,24},{17,... | collective-permute-start | bytes 393224 | tf_op jit(solution)/shard_map/ppermute | solution.py:200
  78.3 3.3 %collective-permute-done.3 = bf16[4,128,128]{2,1,0:T(8,128)(2,1)S(1)} collective-permute-done((bf16[4,128,128]{2,1,0:T(8,128)(2,1)S(1)}, bf16[4,128,128]{2,1,0:T(8,128)(2,1)S(1)}, u32[]{:S(2)}, u32[]{:S(2)}) %collective-permute-start.3) | collective-permute-done | bytes 131104 | tf_op jit(solution)/shard_map/ppermute | solution.py:200
  81.7 0.9 slice_select_fusion
  82.6 1.9 collective-permute-start.4
  84.5 11.3 %collective-permute-done.4 = bf16[4,128,128]{2,1,0:T(8,128)(2,1)S(1)} collective-permute-done((bf16[4,128,128]{2,1,0:T(8,128)(2,1)S(1)}, bf16[4,128,128]{2,1,0:T(8,128)(2,1)S(1)}, u32[]{:S(2)}, u32[]{:S(2)}) %collective-permute-start.4) | collective-permute-done | bytes 131104 | tf_op jit(solution)/shard_map/ppermute | solution.py:203
  95.8 6.6 %collective-permute-done.5 = bf16[4,128,128]{2,1,0:T(8,128)(2,1)S(1)} collective-permute-done((bf16[4,128,128]{2,1,0:T(8,128)(2,1)S(1)}, bf16[4,128,128]{2,1,0:T(8,128)(2,1)S(1)}, u32[]{:S(2)}, u32[]{:S(2)}) %collective-permute-start.5) | collective-permute-done | bytes 131104 | tf_op jit(solution)/shard_map/ppermute | solution.py:204
  102.4 0.7 pad_maximum_fusion.1
  103.1 1.8 broadcast_in_dim.66
  104.9 24.6 %all-to-all-start = ((bf16[16,4,128,128]{3,2,1,0:T(8,128)(2,1)}), bf16[16,4,128,128]{3,2,1,0:T(8,128)(2,1)S(1)}, u32[]{:S(2)}, u32[]{:S(2)}) async-start(bf16[16,4,128,128]{3,2,1,0:T(8,128)(2,1)} %broadcast_in_dim.66), calls=%async_computation | async-start | bytes 4194304 | tf_op jit(solution)/shard_map/all_to_all | solution.py:207
  129.5 26.1 %all-to-all-done.row_half = bf16[16,4,128,128]{3,2,1,0:T(8,128)(2,1)S(1)} async-done(((bf16[16,4,128,128]{3,2,1,0:T(8,128)(2,1)}), bf16[16,4,128,128]{3,2,1,0:T(8,128)(2,1)S(1)}, u32[]{:S(2)}, u32[]{:S(2)}) %all-to-all-start) | async-done | bytes 2097184 | tf_op jit(solution)/shard_map/all_to_all | solution.py:207
  156.4 7.6 %all-to-all-start.1 = ((bf16[16,32,128]{2,1,0:T(8,128)(2,1)}), bf16[16,32,128]{2,1,0:T(8,128)(2,1)S(1)}, u32[]{:S(2)}, u32[]{:S(2)}) async-start(bf16[16,32,128]{2,1,0:T(8,128)(2,1)} %broadcast_in_dim.68), calls=%async_computation.1 | async-start | bytes 262144 | tf_op jit(solution)/shard_map/all_to_all | solution.py:211
  165.4 9.6 %all-to-all-done.1 = bf16[16,32,128]{2,1,0:T(8,128)(2,1)S(1)} async-done(((bf16[16,32,128]{2,1,0:T(8,128)(2,1)}), bf16[16,32,128]{2,1,0:T(8,128)(2,1)S(1)}, u32[]{:S(2)}, u32[]{:S(2)}) %all-to-all-start.1) | async-done | bytes 131104 | tf_op jit(solution)/shard_map/all_to_all | solution.py:211
  175.1 0.9 broadcast_in_dim.69
  176.0 5.2 %all-to-all-start.2 = ((bf16[16,4,32,128]{3,2,1,0:T(8,128)(2,1)}), bf16[16,4,32,128]{3,2,1,0:T(8,128)(2,1)S(1)}, u32[]{:S(2)}, u32[]{:S(2)}) async-start(bf16[16,4,32,128]{3,2,1,0:T(8,128)(2,1)} %broadcast_in_dim.69), calls=%async_computation.2 | async-start | bytes 1048576 | tf_op jit(solution)/shard_map/all_to_all | solution.py:212
  181.6 1.2 select_reduce_fusion
  182.8 1.3 fusion.partner
  184.1 8.8 %assemble.1.front = f32[8,1024,128]{2,1,0:T(8,128)} custom-call(s32[2]{0:T(128)} %pad_add_fusion.place, s32[512]{0:T(512)} %reshape.28.adj, f32[8,1024,128]{2,1,0:T(8,128)} %bitcast.26, bf16[8,4,3,128,128]{4,3,2,1,0:T(8,128)(2,1)} %bitcast.25, bf16[8,2,2,3,128,128]{5,4,3,2,1,0:T(8,128)(2,1)} %bitcast.27), custom_call_target="tpu_custom_call" | custom-call | tf_op jit(solution)/shard_map/assemble/pallas_call | solution.py:216
  193.0 0.8 copy-done.1
  193.8 11.4 %update.1 = f32[8,1024,128]{2,1,0:T(8,128)} custom-call(s32[2]{0:T(128)} %pad_add_fusion.place, s32[256]{0:T(256)} %bitcast.35, f32[8,1024,128]{2,1,0:T(8,128)} %assemble.1.front, bf16[16,4,128,128]{3,2,1,0:T(8,128)(2,1)} %copy-done, bf16[8,2,4,128,128]{4,3,2,1,0:T(8,128)(2,1)} %bitcast.28, bf16[16,4,32,128]{3,2,1,0:T(8,128)(2,1)} %copy-done.1, ...), custom_call_target="tpu_custom_call" | custom-call | tf_op jit(solution)/shard_map/update/pallas_call | solution.py:231
  (38 shorter events, 4.1 us)
Async XLA Ops:
  6.5 27.7 %copy-start.7 = (s32[128,4]{0,1:T(4,128)S(1)}, s32[128,4]{0,1:T(4,128)}, u32[]{:S(2)}) copy-start(s32[128,4]{0,1:T(4,128)} %param.10) | copy-start | bytes 6148
  6.5 177.6 %all-gather.5.cloned.1.call-start = ((), (), s32[]{:S(2)}) async-start(), calls=%async_computation.3 | async-start | bytes 3538944 | tf_op jit(solution)/shard_map/all_gather | solution.py:189
  7.5 11.1 %collective-permute-start = (bf16[2,3,128,128]{3,2,1,0:T(8,128)(2,1)S(1)}, bf16[2,3,128,128]{3,2,1,0:T(8,128)(2,1)S(1)}, u32[]{:S(2)}, u32[]{:S(2)}) collective-permute-start(bf16[2,3,128,128]{3,2,1,0:T(8,128)(2,1)S(1)} %constant_dynamic-slice_fusion), channel_id=1, source_target_pairs={{0,0},{1,16},{2,32},{3,48},{4,64},{5,80},{6,96},{7,112},{8,128},{9... | collective-permute-start | bytes 589832 | tf_op jit(solution)/shard_map/ppermute | solution.py:187
  18.6 10.5 %collective-permute-start.1 = (bf16[2,3,128,128]{3,2,1,0:T(8,128)(2,1)S(1)}, bf16[2,3,128,128]{3,2,1,0:T(8,128)(2,1)S(1)}, u32[]{:S(2)}, u32[]{:S(2)}) collective-permute-start(bf16[2,3,128,128]{3,2,1,0:T(8,128)(2,1)S(1)} %collective-permute-done), channel_id=1, source_target_pairs={{0,16},{16,0},{32,48},{48,32},{64,80},{80,64},{96,112},{112,96},{1... | collective-permute-start | bytes 589832 | tf_op jit(solution)/shard_map/ppermute | solution.py:188
  29.9 163.1 %all-gather.7.cloned.1.call-start = ((), (), s32[]{:S(2)}) async-start(), calls=%async_computation.4 | async-start | bytes 2359296 | tf_op jit(solution)/shard_map/all_gather | solution.py:205
  30.9 35.6 %collective-permute-start.2 = (bf16[4,3,128,128]{3,2,1,0:T(8,128)(2,1)S(1)}, bf16[4,3,128,128]{3,2,1,0:T(8,128)(2,1)S(1)}, u32[]{:S(2)}, u32[]{:S(2)}) collective-permute-start(bf16[4,3,128,128]{3,2,1,0:T(8,128)(2,1)S(1)} %slice_bitcast_fusion), channel_id=1, source_target_pairs={{0,0},{1,16},{2,32},{3,48},{4,64},{5,80},{6,96},{7,112},{8,128},{9... | collective-permute-start | bytes 1179656 | tf_op jit(solution)/shard_map/ppermute | solution.py:183
  66.5 0.8 copy-start.2
  71.2 10.5 %collective-permute-start.3 = (bf16[4,128,128]{2,1,0:T(8,128)(2,1)S(1)}, bf16[4,128,128]{2,1,0:T(8,128)(2,1)S(1)}, u32[]{:S(2)}, u32[]{:S(2)}) collective-permute-start(bf16[4,128,128]{2,1,0:T(8,128)(2,1)S(1)} %slice.30), channel_id=1, source_target_pairs={{0,8},{1,9},{2,10},{3,11},{4,12},{5,13},{6,14},{7,15},{16,24},{17,... | collective-permute-start | bytes 393224 | tf_op jit(solution)/shard_map/ppermute | solution.py:200
  82.6 13.2 %collective-permute-start.4 = (bf16[4,128,128]{2,1,0:T(8,128)(2,1)S(1)}, bf16[4,128,128]{2,1,0:T(8,128)(2,1)S(1)}, u32[]{:S(2)}, u32[]{:S(2)}) collective-permute-start(bf16[4,128,128]{2,1,0:T(8,128)(2,1)S(1)} %slice_select_fusion), channel_id=1, source_target_pairs={{0,0},{1,16},{2,32},{3,48},{4,64},{5,80},{6,96},{7,112},{8,128},{9... | collective-permute-start | bytes 393224 | tf_op jit(solution)/shard_map/ppermute | solution.py:203
  95.8 6.6 %collective-permute-start.5 = (bf16[4,128,128]{2,1,0:T(8,128)(2,1)S(1)}, bf16[4,128,128]{2,1,0:T(8,128)(2,1)S(1)}, u32[]{:S(2)}, u32[]{:S(2)}) collective-permute-start(bf16[4,128,128]{2,1,0:T(8,128)(2,1)S(1)} %collective-permute-done.4), channel_id=1, source_target_pairs={{0,16},{16,0},{32,48},{48,32},{64,80},{80,64},{96,112},{112,96},{1... | collective-permute-start | bytes 393224 | tf_op jit(solution)/shard_map/ppermute | solution.py:204
  104.9 59.0 %copy-start.4 = (f32[2,512]{1,0:T(2,128)S(1)}, f32[2,512]{1,0:T(2,128)}, u32[]{:S(2)}) copy-start(f32[2,512]{1,0:T(2,128)} %param.14) | copy-start | bytes 12292
  104.9 59.0 %copy-start.5 = (s32[2,512]{1,0:T(2,128)S(1)}, s32[2,512]{1,0:T(2,128)}, u32[]{:S(2)}) copy-start(s32[2,512]{1,0:T(2,128)} %param.12) | copy-start | bytes 12292
  104.9 59.2 %copy-start.3 = (s32[2,512]{1,0:T(2,128)S(1)}, s32[2,512]{1,0:T(2,128)}, u32[]{:S(2)}) copy-start(s32[2,512]{1,0:T(2,128)} %param.11) | copy-start | bytes 12292
  104.9 50.7 %all-to-all-start = ((bf16[16,4,128,128]{3,2,1,0:T(8,128)(2,1)}), bf16[16,4,128,128]{3,2,1,0:T(8,128)(2,1)S(1)}, u32[]{:S(2)}, u32[]{:S(2)}) async-start(bf16[16,4,128,128]{3,2,1,0:T(8,128)(2,1)} %broadcast_in_dim.66), calls=%async_computation | async-start | bytes 4194304 | tf_op jit(solution)/shard_map/all_to_all | solution.py:207
  155.7 25.8 %copy-start = (bf16[16,4,128,128]{3,2,1,0:T(8,128)(2,1)}, bf16[16,4,128,128]{3,2,1,0:T(8,128)(2,1)S(1)}, u32[]{:S(2)}) copy-start(bf16[16,4,128,128]{3,2,1,0:T(8,128)(2,1)S(1)} %all-to-all-done.row_half) | copy-start | bytes 6291460
  155.7 25.9 %copy-start.6 = (f32[2,512]{1,0:T(2,128)S(1)}, f32[2,512]{1,0:T(2,128)}, u32[]{:S(2)}) copy-start(f32[2,512]{1,0:T(2,128)} %param.13) | copy-start | bytes 12292
  156.4 18.7 %all-to-all-start.1 = ((bf16[16,32,128]{2,1,0:T(8,128)(2,1)}), bf16[16,32,128]{2,1,0:T(8,128)(2,1)S(1)}, u32[]{:S(2)}, u32[]{:S(2)}) async-start(bf16[16,32,128]{2,1,0:T(8,128)(2,1)} %broadcast_in_dim.68), calls=%async_computation.1 | async-start | bytes 262144 | tf_op jit(solution)/shard_map/all_to_all | solution.py:211
  176.0 17.0 %all-to-all-start.2 = ((bf16[16,4,32,128]{3,2,1,0:T(8,128)(2,1)}), bf16[16,4,32,128]{3,2,1,0:T(8,128)(2,1)S(1)}, u32[]{:S(2)}, u32[]{:S(2)}) async-start(bf16[16,4,32,128]{3,2,1,0:T(8,128)(2,1)} %broadcast_in_dim.69), calls=%async_computation.2 | async-start | bytes 1048576 | tf_op jit(solution)/shard_map/all_to_all | solution.py:212
  193.0 0.8 copy-start.1
Sparse Core Ops, SparseCore 0:
  30.0 62.1 all-gather.4
  103.2 58.1 all-gather.6

commit v2 on v1

v2 whole, which is shorter than its diff:
```python
import jax
import jax.numpy as jnp
from jax import lax
from jax.experimental import pallas as pl
from jax.experimental.pallas import tpu as pltpu
from jax.sharding import PartitionSpec as P


NB = 128
PW = 512
N = 16
BOTH = ("row", "col")
F32 = jnp.float32
BF16 = jnp.bfloat16

SWAP_X = [(r, r ^ 1) for r in range(N)]
Z_LINES = [[2 * z + x for z in range(8)] for x in (0, 1)]


def spread_target(q, j):
    return 2 * ((q // 2 + j // 2) % 8) + j % 2


SPREAD = [(q * N + j, spread_target(q, j) * N + q) for q in range(N) for j in range(N)]
SPREAD_A = [(s, d) for s, d in SPREAD if s % N < 8]
SPREAD_B = [(s - 8, d) for s, d in SPREAD if s % N >= 8]
HALVE = [(n, n + 8) for n in range(8)]
SWAP_CORE = [(c, c ^ 1) for c in range(N)]
SAME_CORE = [[2 * i + k for i in range(8)] for k in (0, 1)]


def left_of(ref, lead):
    v, s, l = ref[lead + (0,)], ref[lead + (1,)], ref[lead + (2,)]
    return jnp.concatenate([v, v, s, l], axis=0)


def right_of_parts(v, s, l):
    return jnp.concatenate([v * 4.0, s * -0.5, v * -0.5, l * 2.0], axis=0).astype(BF16)


def right_of(ref, lead):
    return right_of_parts(ref[lead + (0,)], ref[lead + (1,)], ref[lead + (2,)])


def right_of_chunks(chunks):
    rows = jnp.concatenate(chunks, axis=0)
    return right_of_parts(rows[:NB], rows[NB : 2 * NB], rows[2 * NB :])


def pair_product(left, right):
    return lax.dot_general(left, right, (((0,), (0,)), ((), ())), preferred_element_type=F32)


def panel_block_kernel(place, adj, base, own, faces, lower, upper, acc):
    r, c = place[0], place[1]
    acc[...] = base[...]
    for g in range(4):
        e = adj[c * 4 + g]

        @pl.when((e % N == r) & (c < 8))
        def _():
            a = e // N
            right = right_of_chunks([faces[2 * (4 * (g % 2) + k) + g // 2] for k in range(4)])
            acc[a] -= pair_product(left_of(own, (a, g ^ 1)), right)

    @pl.when(r == c)
    def _():
        for f in range(4):
            acc[0] += pair_product(left_of(own, (0, f)), right_of(own, (0, f)))

    lower[...] = acc[:4].astype(BF16)
    upper[...] = acc[4:].astype(BF16)


def couple(place, adj, own, faces, out, t, a, parity):
    r, c = place[0], place[1]
    for f in (0, 1) if parity == 0 else (2, 3):
        n = adj[(a * N + r) * 4 + f]

        @pl.when(n % N == c)
        def _():
            b = n // N
            right = right_of_chunks([faces[4 * (1 - f % 2) + k, b] for k in range(4)])
            rows = pl.ds(b, NB, stride=8)
            out[t, rows, :] = out[t, rows, :] - pair_product(left_of(own, (t, f)), right)


def assemble_kernel(place, adj, base, own, faces, out):
    r, c = place[0], place[1]
    a = pl.program_id(0)
    out[...] = base[...]
    for parity in (0, 1):
        pl.when(r % 2 == parity)(lambda: couple(place, adj, own, faces, out, 0, a, parity))

    @pl.when(r == c)
    def _():
        total = pair_product(left_of(own, (0, 0)), right_of(own, (0, 0)))
        for f in range(1, 4):
            total += pair_product(left_of(own, (0, f)), right_of(own, (0, f)))
        rows = pl.ds(a, NB, stride=8)
        out[0, rows, :] = out[0, rows, :] + total


def dot_nt(x, y):
    return lax.dot_general(x, y, (((1,), (1,)), ((), ())), preferred_element_type=F32)


def scale(values, partner, diag, side):
    swapped = jnp.dot(values, partner, preferred_element_type=F32)
    return (values.astype(F32) * diag + swapped * side).astype(BF16)


def keep(readers, k, e):
    return jnp.where((readers[k * 128 + e] == 1) & (e >= 4 * (k + 1)), 1.0, 0.0).astype(F32)


def row_side_kernel(place, readers, row_own, row_other, partner, diag, side, w0r, w1r, cross, v0r, f1r):
    r, c = place[0], place[1]
    step = pl.program_id(0)

    def tile_of(n, chunk, slot):
        at = (n // 2 + 4 * chunk, slot)
        return jnp.where(c % 2 == n % 2, row_own[at], row_other[at])

    @pl.when(step == 0)
    def _():
        for i in range(4):
            kept = keep(readers, 0, 4 + i)
            for n in range(4):
                tile = tile_of(n, i // 2, 4 + i % 2).astype(F32) * kept
                cross[i * NB : (i + 1) * NB, n * NB : (n + 1) * NB] = tile.astype(BF16)

    for t in range(2):
        a = 2 * step + t
        kept = keep(readers, 0, a * N + r)
        rows = slice(t * NB, (t + 1) * NB)
        for n in range(8):
            tile = tile_of(n, a // 4, a % 4)
            if n < 4:
                v0r[rows, n * NB : (n + 1) * NB] = (tile.astype(F32) * kept).astype(BF16)
            else:
                f1r[rows, (n - 4) * NB : (n - 3) * NB] = tile
    w0 = scale(v0r[...], partner[0], diag[0:1], side[0:1])
    w0r[...] = w0
    fresh = f1r[...].astype(F32) - dot_nt(w0, cross[...])
    for t in range(2):
        kept = keep(readers, 1, (2 * step + t) * N + r)
        f1r[t * NB : (t + 1) * NB, :] = (fresh[t * NB : (t + 1) * NB] * kept).astype(BF16)
    w1r[...] = scale(f1r[...], partner[1], diag[1:2], side[1:2])


def update_kernel(
    place, adj, readers, front, own, faces_x, w0r, w1r, cross, col_half, partner, diag, side, out, v0c, v1c,
):
    r, c = place[0], place[1]
    step = pl.program_id(0)

    @pl.when(step == 0)
    def _():
        for b in range(8):
            kept = keep(readers, 0, b * N + c)
            for n in range(8):
                j = n + 8 * (b // 4)
                tile = col_half[(j // 2 + c // 2) % 8, (j % 2) ^ (r % 2), b % 4]
                rows = slice(b * NB, (b + 1) * NB)
                if n < 4:
                    v0c[rows, n * NB : (n + 1) * NB] = (tile.astype(F32) * kept).astype(BF16)
                else:
                    v1c[rows, (n - 4) * NB : (n - 3) * NB] = tile
        w0c = scale(v0c[...], partner[0], diag[0:1], side[0:1])
        fresh = v1c[...].astype(F32) - dot_nt(w0c, cross[...])
        for b in range(8):
            kept = keep(readers, 1, b * N + c)
            v1c[b * NB : (b + 1) * NB, :] = (fresh[b * NB : (b + 1) * NB] * kept).astype(BF16)

    change = dot_nt(w0r[...], v0c[...]) + dot_nt(w1r[...], v1c[...])
    for t in range(2):
        for b in range(8):
            rows = pl.ds(b, NB, stride=8)
            out[t, rows, :] = front[t, rows, :] - change[t * NB : (t + 1) * NB, b * NB : (b + 1) * NB]
        for parity in (0, 1):
            pl.when(r % 2 != parity)(lambda: couple(place, adj, own, faces_x, out, t, 2 * step + t, parity))


def pivot_tables(pivot_order, pivot_kind, inverse_diagonal, inverse_coupling):
    at = pivot_order[:, :, None] == jnp.arange(PW, dtype=jnp.int32)[None, None, :]
    starts = jnp.where(pivot_kind == 1, inverse_coupling, 0.0).reshape(2, PW // 2, 2)[:, :, 0]
    factor = jnp.repeat(starts, 2, axis=1)
    diag = jnp.sum(jnp.where(at, inverse_diagonal[:, :, None], 0.0), axis=1)
    side = jnp.sum(jnp.where(at, factor[:, :, None], 0.0), axis=1)
    order_swapped = pivot_order.reshape(2, PW // 2, 2)[:, :, ::-1].reshape(2, PW)
    partner_of = jnp.sum(jnp.where(at, order_swapped[:, :, None], 0), axis=1)
    partner = (jnp.arange(PW, dtype=jnp.int32)[None, :, None] == partner_of[:, None, :]).astype(BF16)
    return partner, diag, side


def smem():
    return pl.BlockSpec(memory_space=pltpu.SMEM)


def vmem():
    return pl.BlockSpec(memory_space=pltpu.VMEM)


def steps(
    front_base, traces, adjacency, pivot_order, pivot_kind, inverse_diagonal, inverse_coupling, readers,
):
    r = lax.axis_index("row")
    c = lax.axis_index("col")
    place = jnp.stack([r, c]).astype(jnp.int32)
    adj = adjacency.reshape(-1)
    own = traces[:, 0]
    base = front_base.reshape(8, 8 * NB, NB)

    chunk = (r // 2 + c // 2) % 8 + 8 * (c % 2)
    piece = lax.dynamic_index_in_dim(own.reshape(8, N, 96, NB), chunk, 1, keepdims=False)
    piece = lax.ppermute(piece, BOTH, SPREAD)
    faces = lax.all_gather(piece, "row", axis=0, axis_index_groups=Z_LINES)
    faces_x = lax.ppermute(faces, "row", SWAP_X)
    low_faces = lax.all_to_all(jnp.broadcast_to(piece[:1], (N, 96, NB)), "row", 0, 0, tiled=True)

    base_low = front_base[:, 0, :, 0, 0, :]
    lower, upper = pl.pallas_call(
        panel_block_kernel,
        out_shape=(jax.ShapeDtypeStruct((4, NB, NB), BF16),) * 2,
        in_specs=[smem(), smem(), vmem(), vmem(), vmem()],
        out_specs=(vmem(), vmem()),
        scratch_shapes=[pltpu.VMEM((8, NB, NB), F32)],
        name="panel_block",
    )(place, adj, base_low, own, low_faces)

    spread_a = lax.ppermute(lower, BOTH, SPREAD_A)
    spread_b = lax.ppermute(upper, BOTH, SPREAD_B)
    spread = jnp.where((r // 2 - c // 2) % 8 < 4, spread_a, spread_b)
    other = lax.ppermute(spread, "row", SWAP_X)
    pair = jnp.stack([spread, other])
    col_half = lax.all_gather(pair, "row", axis=0, axis_index_groups=Z_LINES)

    cross_row = lax.all_to_all(jnp.broadcast_to(lower[:1], (N, NB, NB)), "row", 0, 0, tiled=True)[4:8]

    moved = lax.ppermute(jnp.concatenate([upper, cross_row[2:]]), "col", HALVE)
    half = jnp.where(c < 8, jnp.concatenate([lower, cross_row[:2]]), moved)
    row_own = lax.all_to_all(
        jnp.broadcast_to(half[None], (8,) + half.shape), "col", 0, 0, tiled=True, axis_index_groups=SAME_CORE
    )
    row_other = lax.ppermute(row_own, "col", SWAP_CORE)

    partner, diag, side = pivot_tables(pivot_order, pivot_kind, inverse_diagonal, inverse_coupling)

    front = pl.pallas_call(
        assemble_kernel,
        grid=(8,),
        out_shape=jax.ShapeDtypeStruct((8, 8 * NB, NB), F32),
        in_specs=[
            smem(),
            smem(),
            pl.BlockSpec((1, 8 * NB, NB), lambda a: (a, 0, 0)),
            pl.BlockSpec((1, 4, 3, NB, NB), lambda a: (a, 0, 0, 0, 0)),
            vmem(),
        ],
        out_specs=pl.BlockSpec((1, 8 * NB, NB), lambda a: (a, 0, 0)),
        name="assemble",
    )(place, adj, base, own, faces)

    by_two = pl.BlockSpec((2 * NB, PW), lambda s: (s, 0))
    w0r, w1r, cross = pl.pallas_call(
        row_side_kernel,
        grid=(4,),
        out_shape=(jax.ShapeDtypeStruct((8 * NB, PW), BF16),) * 2 + (jax.ShapeDtypeStruct((PW, PW), BF16),),
        in_specs=[smem(), smem(), vmem(), vmem(), vmem(), vmem(), vmem()],
        out_specs=(by_two, by_two, pl.BlockSpec((PW, PW), lambda s: (0, 0))),
        scratch_shapes=[pltpu.VMEM((2 * NB, PW), BF16), pltpu.VMEM((2 * NB, PW), BF16)],
        name="row_side",
    )(place, readers.reshape(-1), row_own, row_other, partner, diag, side)

    out = pl.pallas_call(
        update_kernel,
        grid=(4,),
        out_shape=jax.ShapeDtypeStruct((8, 8 * NB, NB), F32),
        in_specs=[
            smem(),
            smem(),
            smem(),
            pl.BlockSpec((2, 8 * NB, NB), lambda s: (s, 0, 0)),
            pl.BlockSpec((2, 4, 3, NB, NB), lambda s: (s, 0, 0, 0, 0)),
            vmem(),
            by_two,
            by_two,
            vmem(),
            vmem(),
            vmem(),
            vmem(),
            vmem(),
        ],
        out_specs=pl.BlockSpec((2, 8 * NB, NB), lambda s: (s, 0, 0)),
        scratch_shapes=[pltpu.VMEM((8 * NB, PW), BF16), pltpu.VMEM((8 * NB, PW), BF16)],
        name="update",
    )(place, adj, readers.reshape(-1), front, own, faces_x, w0r, w1r, cross, col_half, partner, diag, side)
    return out.reshape(8, 1, NB, 8, 1, NB)


def solution(mesh):
    in_specs = (
        P(None, "row", None, None, "col", None),
        P(None, "row", None, None, None, None),
        P(),
        P(),
        P(),
        P(),
        P(),
        P(),
    )
    out_specs = P(None, "row", None, None, "col", None)
    return jax.shard_map(steps, mesh=mesh, in_specs=in_specs, out_specs=out_specs, check_vma=False)
```

time: 214 us -> 196 us (0.916)
  waiting for transfers between devices: 95.9 us -> 55 us
  blocking collectives: 0 us -> 29.6 us
  starting transfers between devices: 61.3 us -> 48.2 us
  Pallas kernels: 23.2 us -> 28.4 us
  local copies, waits for them, and re-layouts: 11.9 us -> 14.2 us
    all_to_all x0 -> x1, blocking collectives: none -> 29.6 us  [steps(): lax.all_to_all(jnp.broadcast_to(half[None], (8,) + half.shape), 'col', 0,...]
    ppermute x6 -> x7, waiting for transfers between devices: 60.1 us -> 39.5 us  [the longest x1 16.5 us: steps(): faces_x = lax.ppermute(faces, 'row', SWAP_X)]
    all_to_all x3 -> x2, waiting for transfers between devices: 35.8 us -> 15.5 us  [the longest x1 15.5 us: steps(): lax.all_to_all(jnp.broadcast_to(piece[:1], (N, 96, NB)), 'row', 0, 0, til...]
    all_to_all x3 -> x2, starting transfers between devices: 37.3 us -> 22.9 us  [the longest x1 19.3 us: steps(): lax.all_to_all(jnp.broadcast_to(piece[:1], (N, 96, NB)), 'row', 0, 0, til...]
    pallas_call x3 -> x4, Pallas kernels: 23.2 us -> 28.4 us  [the longest x1 11.3 us: steps(): pl.pallas_call(update_kernel, grid=(4,), out_shape=jax.ShapeDtypeStruct((...]
    ppermute x6 -> x7, starting transfers between devices: 23.9 us -> 25.2 us  [the longest x1 11.3 us: steps(): spread_b = lax.ppermute(upper, BOTH, SPREAD_B)]
  transfers between devices with their start and end apart: 11 -> 11, of which waited for: 8 -> 6; matrix products, arithmetic and copies ran while one was open for 7% -> 8% of each run, Pallas kernels for 6% -> 9%
where the time goes in v2:
time: 196 us; the launch traced here: 193 us
  waiting for transfers between devices  55 us (28%)
  starting transfers between devices  48.2 us (25%)
  blocking collectives  29.6 us (15%)
  Pallas kernels  28.4 us (14%)
  local copies, waits for them, and re-layouts  14.2 us (7%)
  between operations  13.7 us (7%)
  other arithmetic  4.4 us (2%)
    all_to_all x1, blocking collectives, steps(): lax.all_to_all(jnp.broadcast_to(half[None], (8,) + half.shape), 'col', 0,...  29.6 us
    all_to_all x1, starting transfers between devices, steps(): lax.all_to_all(jnp.broadcast_to(piece[:1], (N, 96, NB)), 'row', 0, 0, til...  19.3 us
    ppermute x1, waiting for transfers between devices, steps(): faces_x = lax.ppermute(faces, 'row', SWAP_X)  16.5 us
    all_to_all x1, waiting for transfers between devices, steps(): lax.all_to_all(jnp.broadcast_to(piece[:1], (N, 96, NB)), 'row', 0, 0, til...  15.5 us
    pallas_call x1, Pallas kernels, steps(): pl.pallas_call(update_kernel, grid=(4,), out_shape=jax.ShapeDtypeStruct((...  11.3 us
    ppermute x1, starting transfers between devices, steps(): spread_b = lax.ppermute(upper, BOTH, SPREAD_B)  11.3 us
    ppermute x1, waiting for transfers between devices, steps(): spread_b = lax.ppermute(upper, BOTH, SPREAD_B)  8.44 us
    pallas_call x1, Pallas kernels, steps(): pl.pallas_call(assemble_kernel, grid=(8,), out_shape=jax.ShapeDtypeStruct...  8.11 us
  transfers between devices with their start and end apart: 11, of which 6 were waited for; matrix products, arithmetic and copies ran while one was open for 8% of the time, Pallas kernels for 9%

profile of v2, /device:TPU:8, one launch (start us, length us, event | category | flops | bytes accessed | tf_op | source)
XLA Modules:
  0.0 193.4 jit_solution(6600310454707902481)
XLA Ops:
  6.5 0.9 dynamic-slice_bitcast_fusion
  7.5 5.1 %collective-permute-start = (bf16[8,96,128]{2,1,0:T(8,128)(2,1)S(1)}, bf16[8,96,128]{2,1,0:T(8,128)(2,1)S(1)}, u32[]{:S(2)}, u32[]{:S(2)}) collective-permute-start(bf16[8,96,128]{2,1,0:T(8,128)(2,1)S(1)} %dynamic-slice_bitcast_fusion), channel_id=1, source_target_pairs={{0,0},{1,16},{2,32},{3,48},{4,64},{5,80},{6,96},{7,112},{8,128},{9... | collective-permute-start | bytes 589832 | tf_op jit(solution)/shard_map/ppermute | solution.py:217
  12.6 6.0 %collective-permute-done = bf16[8,96,128]{2,1,0:T(8,128)(2,1)S(1)} collective-permute-done((bf16[8,96,128]{2,1,0:T(8,128)(2,1)S(1)}, bf16[8,96,128]{2,1,0:T(8,128)(2,1)S(1)}, u32[]{:S(2)}, u32[]{:S(2)}) %collective-permute-start) | collective-permute-done | bytes 196640 | tf_op jit(solution)/shard_map/ppermute | solution.py:217
  19.3 0.7 slice_bitcast_fusion.1
  20.0 0.8 broadcast_in_dim.67
  20.8 19.3 %all-to-all-start = ((bf16[16,96,128]{2,1,0:T(8,128)(2,1)}), bf16[16,96,128]{2,1,0:T(8,128)(2,1)S(1)}, u32[]{:S(2)}, u32[]{:S(2)}) async-start(bf16[16,96,128]{2,1,0:T(8,128)(2,1)} %broadcast_in_dim.67), calls=%async_computation | async-start | bytes 786432 | tf_op jit(solution)/shard_map/all_to_all | solution.py:220
  40.1 0.8 copy.18
  41.6 1.9 slice.21
  44.2 15.5 %all-to-all-done.faces = bf16[16,96,128]{2,1,0:T(8,128)(2,1)S(1)} async-done(((bf16[16,96,128]{2,1,0:T(8,128)(2,1)}), bf16[16,96,128]{2,1,0:T(8,128)(2,1)S(1)}, u32[]{:S(2)}, u32[]{:S(2)}) %all-to-all-start) | async-done | bytes 393248 | tf_op jit(solution)/shard_map/all_to_all | solution.py:220
  59.6 0.7 copy-done.2
  60.4 2.9 %panel_block.1 = (bf16[4,128,128]{2,1,0:T(8,128)(2,1)}, bf16[4,128,128]{2,1,0:T(8,128)(2,1)}) custom-call(s32[2]{0:T(128)} %pad_add_fusion.place, s32[512]{0:T(512)} %reshape.25.adj, f32[8,128,128]{2,1,0:T(8,128)} %bitcast.29, bf16[8,4,3,128,128]{4,3,2,1,0:T(8,128)(2,1)} %bitcast.25, bf16[16,96,128]{2,1,0:T(8,128)(2,1)} %copy-done.2), custom_call_target="tpu_custom_call" | custom-call | tf_op jit(solution)/shard_map/panel_block/pallas_call | solution.py:223
  63.3 0.8 slice_bitcast_fusion
  64.1 0.9 broadcast_in_dim.69
  65.0 3.6 %all-to-all-start.1 = ((bf16[16,128,128]{2,1,0:T(8,128)(2,1)}), bf16[16,128,128]{2,1,0:T(8,128)(2,1)S(1)}, u32[]{:S(2)}, u32[]{:S(2)}) async-start(bf16[16,128,128]{2,1,0:T(8,128)(2,1)} %broadcast_in_dim.69), calls=%async_computation.1 | async-start | bytes 1048576 | tf_op jit(solution)/shard_map/all_to_all | solution.py:239
  68.6 11.3 %collective-permute-start.5 = (bf16[4,128,128]{2,1,0:T(8,128)(2,1)}, bf16[4,128,128]{2,1,0:T(8,128)(2,1)S(1)}, u32[]{:S(2)}, u32[]{:S(2)}) collective-permute-start(bf16[4,128,128]{2,1,0:T(8,128)(2,1)} %get-tuple-element.11), channel_id=1, source_target_pairs={{0,128},{1,144},{2,160},{3,176},{4,192},{5,208},{6,224},{7,240},{1... | collective-permute-start | bytes 393224 | tf_op jit(solution)/shard_map/ppermute | solution.py:233
  79.9 1.3 collective-permute-start.4
  81.2 8.4 %collective-permute-done.5 = bf16[4,128,128]{2,1,0:T(8,128)(2,1)S(1)} collective-permute-done((bf16[4,128,128]{2,1,0:T(8,128)(2,1)}, bf16[4,128,128]{2,1,0:T(8,128)(2,1)S(1)}, u32[]{:S(2)}, u32[]{:S(2)}) %collective-permute-start.5) | collective-permute-done | bytes 131104 | tf_op jit(solution)/shard_map/ppermute | solution.py:233
  89.7 2.3 %collective-permute-start.6 = (bf16[4,128,128]{2,1,0:T(8,128)(2,1)S(1)}, bf16[4,128,128]{2,1,0:T(8,128)(2,1)S(1)}, u32[]{:S(2)}, u32[]{:S(2)}) collective-permute-start(bf16[4,128,128]{2,1,0:T(8,128)(2,1)S(1)} %broadcast_select_fusion), channel_id=1, source_target_pairs={{0,16},{16,0},{32,48},{48,32},{64,80},{80,64},{96,112},{112,96},{1... | collective-permute-start | bytes 393224 | tf_op jit(solution)/shard_map/ppermute | solution.py:235
  92.0 4.2 %collective-permute-done.6 = bf16[4,128,128]{2,1,0:T(8,128)(2,1)S(1)} collective-permute-done((bf16[4,128,128]{2,1,0:T(8,128)(2,1)S(1)}, bf16[4,128,128]{2,1,0:T(8,128)(2,1)S(1)}, u32[]{:S(2)}, u32[]{:S(2)}) %collective-permute-start.6) | collective-permute-done | bytes 131104 | tf_op jit(solution)/shard_map/ppermute | solution.py:235
  96.3 0.7 pad_maximum_fusion
  97.1 5.2 %collective-permute-start.2 = (bf16[6,128,128]{2,1,0:T(8,128)(2,1)S(1)}, bf16[6,128,128]{2,1,0:T(8,128)(2,1)S(1)}, u32[]{:S(2)}, u32[]{:S(2)}) collective-permute-start(bf16[6,128,128]{2,1,0:T(8,128)(2,1)S(1)} %pad_maximum_fusion.1), channel_id=1, source_target_pairs={{0,8},{1,9},{2,10},{3,11},{4,12},{5,13},{6,14},{7,15},{16,24},{17,... | collective-permute-start | bytes 589832 | tf_op jit(solution)/shard_map/ppermute | solution.py:241
  102.3 4.3 %collective-permute-done.2 = bf16[6,128,128]{2,1,0:T(8,128)(2,1)S(1)} collective-permute-done((bf16[6,128,128]{2,1,0:T(8,128)(2,1)S(1)}, bf16[6,128,128]{2,1,0:T(8,128)(2,1)S(1)}, u32[]{:S(2)}, u32[]{:S(2)}) %collective-permute-start.2) | collective-permute-done | bytes 196640 | tf_op jit(solution)/shard_map/ppermute | solution.py:241
  107.1 29.6 %all_to_all.15.row_own = bf16[8,6,128,128]{3,2,1,0:T(8,128)(2,1)S(1)} all-to-all(bf16[8,6,128,128]{3,2,1,0:T(8,128)(2,1)S(1)} %broadcast_in_dim.70), channel_id=1, replica_groups={{0,2,4,6,8,10,12,14},{1,3,5,7,9,11,13,15},{16,18,20,22,24,26,28,30},{17..., dimensions={0} | all-to-all | bytes 3145728 | tf_op jit(solution)/shard_map/all_to_all | solution.py:243
  137.5 0.9 reshape.28
  138.4 1.9 rev.3
  141.0 1.2 select_reduce_fusion
  142.2 1.3 fusion.partner
  143.5 8.1 %assemble.1.front = f32[8,1024,128]{2,1,0:T(8,128)} custom-call(s32[2]{0:T(128)} %pad_add_fusion.place, s32[512]{0:T(512)} %reshape.25.adj, f32[8,1024,128]{2,1,0:T(8,128)} %bitcast.28, bf16[8,4,3,128,128]{4,3,2,1,0:T(8,128)(2,1)} %bitcast.26, bf16[8,8,96,128]{3,2,1,0:T(8,128)(2,1)} %bitcast.32), custom_call_target="tpu_custom_call" | custom-call | tf_op jit(solution)/shard_map/assemble/pallas_call | solution.py:250
  151.6 1.1 copy-done.1
  152.7 6.1 %row_side.1 = (bf16[1024,512]{1,0:T(8,128)(2,1)}, bf16[1024,512]{1,0:T(8,128)(2,1)}, bf16[512,512]{1,0:T(8,128)(2,1)}) custom-call(s32[2]{0:T(128)} %pad_add_fusion.place, s32[256]{0:T(256)} %bitcast.35, bf16[8,6,128,128]{3,2,1,0:T(8,128)(2,1)} %copy-done, bf16[8,6,128,128]{3,2,1,0:T(8,128)(2,1)} %copy-done.1, bf16[2,512,512]{2,1,0:T(8,128)(2,1)} %fusion.partner, ...), custom_call_target="tpu_custom_call" | custom-call | tf_op jit(solution)/shard_map/row_side/pallas_call | solution.py:266
  158.8 16.5 %collective-permute-done.1.faces_x = bf16[8,8,96,128]{3,2,1,0:T(8,128)(2,1)} collective-permute-done((bf16[8,8,96,128]{3,2,1,0:T(8,128)(2,1)}, bf16[8,8,96,128]{3,2,1,0:T(8,128)(2,1)}, u32[]{:S(2)}, u32[]{:S(2)}) %collective-permute-start.1) | collective-permute-done | bytes 1572896 | tf_op jit(solution)/shard_map/ppermute | solution.py:219
  175.3 11.3 %update.1 = f32[8,1024,128]{2,1,0:T(8,128)} custom-call(s32[2]{0:T(128)} %pad_add_fusion.place, s32[512]{0:T(512)} %reshape.25.adj, s32[256]{0:T(256)} %bitcast.36, f32[8,1024,128]{2,1,0:T(8,128)} %assemble.1.front, bf16[8,4,3,128,128]{4,3,2,1,0:T(8,128)(2,1)} %bitcast.27, bf16[8,8,96,128]{3,2,1,0:T(8,128)(2,1)} %collective-permute-done.1.faces_x, ...), custom_call_target="tpu_custom_call" | custom-call | tf_op jit(solution)/shard_map/update/pallas_call | solution.py:276
  (43 shorter events, 4.0 us)
Async XLA Ops:
  6.5 130.1 %all-gather.5.cloned.1.call-start = ((), (), s32[]{:S(2)}) async-start(), calls=%async_computation.3 | async-start | bytes 1769472 | tf_op jit(solution)/shard_map/all_gather | solution.py:218
  7.5 11.1 %collective-permute-start = (bf16[8,96,128]{2,1,0:T(8,128)(2,1)S(1)}, bf16[8,96,128]{2,1,0:T(8,128)(2,1)S(1)}, u32[]{:S(2)}, u32[]{:S(2)}) collective-permute-start(bf16[8,96,128]{2,1,0:T(8,128)(2,1)S(1)} %dynamic-slice_bitcast_fusion), channel_id=1, source_target_pairs={{0,0},{1,16},{2,32},{3,48},{4,64},{5,80},{6,96},{7,112},{8,128},{9... | collective-permute-start | bytes 589832 | tf_op jit(solution)/shard_map/ppermute | solution.py:217
  18.6 0.7 copy-start.3
  20.8 38.8 %all-to-all-start = ((bf16[16,96,128]{2,1,0:T(8,128)(2,1)}), bf16[16,96,128]{2,1,0:T(8,128)(2,1)S(1)}, u32[]{:S(2)}, u32[]{:S(2)}) async-start(bf16[16,96,128]{2,1,0:T(8,128)(2,1)} %broadcast_in_dim.67), calls=%async_computation | async-start | bytes 786432 | tf_op jit(solution)/shard_map/all_to_all | solution.py:220
  59.6 0.7 copy-start.2
  63.3 33.8 %copy-start.5 = (bf16[4,128,128]{2,1,0:T(8,128)(2,1)S(1)}, bf16[4,128,128]{2,1,0:T(8,128)(2,1)}, u32[]{:S(2)}) copy-start(bf16[4,128,128]{2,1,0:T(8,128)(2,1)} %get-tuple-element.11) | copy-start | bytes 393220
  63.3 43.3 %copy-start.4 = (bf16[4,128,128]{2,1,0:T(8,128)(2,1)S(1)}, bf16[4,128,128]{2,1,0:T(8,128)(2,1)}, u32[]{:S(2)}) copy-start(bf16[4,128,128]{2,1,0:T(8,128)(2,1)} %get-tuple-element.10) | copy-start | bytes 393220
  65.0 32.0 %all-to-all-start.1 = ((bf16[16,128,128]{2,1,0:T(8,128)(2,1)}), bf16[16,128,128]{2,1,0:T(8,128)(2,1)S(1)}, u32[]{:S(2)}, u32[]{:S(2)}) async-start(bf16[16,128,128]{2,1,0:T(8,128)(2,1)} %broadcast_in_dim.69), calls=%async_computation.1 | async-start | bytes 1048576 | tf_op jit(solution)/shard_map/all_to_all | solution.py:239
  68.6 106.7 %all-gather.7.cloned.1.call-start = ((), (), s32[]{:S(2)}) async-start(), calls=%async_computation.4 | async-start | bytes 2359296 | tf_op jit(solution)/shard_map/all_gather | solution.py:237
  68.6 21.0 %collective-permute-start.5 = (bf16[4,128,128]{2,1,0:T(8,128)(2,1)}, bf16[4,128,128]{2,1,0:T(8,128)(2,1)S(1)}, u32[]{:S(2)}, u32[]{:S(2)}) collective-permute-start(bf16[4,128,128]{2,1,0:T(8,128)(2,1)} %get-tuple-element.11), channel_id=1, source_target_pairs={{0,128},{1,144},{2,160},{3,176},{4,192},{5,208},{6,224},{7,240},{1... | collective-permute-start | bytes 393224 | tf_op jit(solution)/shard_map/ppermute | solution.py:233
  79.9 9.8 %collective-permute-start.4 = (bf16[4,128,128]{2,1,0:T(8,128)(2,1)}, bf16[4,128,128]{2,1,0:T(8,128)(2,1)S(1)}, u32[]{:S(2)}, u32[]{:S(2)}) collective-permute-start(bf16[4,128,128]{2,1,0:T(8,128)(2,1)} %get-tuple-element.10), channel_id=1, source_target_pairs={{0,0},{1,16},{2,32},{3,48},{4,64},{5,80},{6,96},{7,112},{16,1},{17... | collective-permute-start | bytes 393224 | tf_op jit(solution)/shard_map/ppermute | solution.py:232
  89.7 6.6 %collective-permute-start.6 = (bf16[4,128,128]{2,1,0:T(8,128)(2,1)S(1)}, bf16[4,128,128]{2,1,0:T(8,128)(2,1)S(1)}, u32[]{:S(2)}, u32[]{:S(2)}) collective-permute-start(bf16[4,128,128]{2,1,0:T(8,128)(2,1)S(1)} %broadcast_select_fusion), channel_id=1, source_target_pairs={{0,16},{16,0},{32,48},{48,32},{64,80},{80,64},{96,112},{112,96},{1... | collective-permute-start | bytes 393224 | tf_op jit(solution)/shard_map/ppermute | solution.py:235
  97.1 9.5 %collective-permute-start.2 = (bf16[6,128,128]{2,1,0:T(8,128)(2,1)S(1)}, bf16[6,128,128]{2,1,0:T(8,128)(2,1)S(1)}, u32[]{:S(2)}, u32[]{:S(2)}) collective-permute-start(bf16[6,128,128]{2,1,0:T(8,128)(2,1)S(1)} %pad_maximum_fusion.1), channel_id=1, source_target_pairs={{0,8},{1,9},{2,10},{3,11},{4,12},{5,13},{6,14},{7,15},{16,24},{17,... | collective-permute-start | bytes 589832 | tf_op jit(solution)/shard_map/ppermute | solution.py:241
  106.6 30.1 %copy-start.7 = (f32[2,512]{1,0:T(2,128)S(1)}, f32[2,512]{1,0:T(2,128)}, u32[]{:S(2)}) copy-start(f32[2,512]{1,0:T(2,128)} %param.14) | copy-start | bytes 12292
  106.7 30.1 %copy-start.8 = (s32[2,512]{1,0:T(2,128)S(1)}, s32[2,512]{1,0:T(2,128)}, u32[]{:S(2)}) copy-start(s32[2,512]{1,0:T(2,128)} %param.12) | copy-start | bytes 12292
  107.0 30.5 %copy-start.6 = (s32[2,512]{1,0:T(2,128)S(1)}, s32[2,512]{1,0:T(2,128)}, u32[]{:S(2)}) copy-start(s32[2,512]{1,0:T(2,128)} %param.11) | copy-start | bytes 12292
  107.0 33.9 %copy-start.9 = (f32[2,512]{1,0:T(2,128)S(1)}, f32[2,512]{1,0:T(2,128)}, u32[]{:S(2)}) copy-start(f32[2,512]{1,0:T(2,128)} %param.13) | copy-start | bytes 12292
  136.7 14.9 %copy-start = (bf16[8,6,128,128]{3,2,1,0:T(8,128)(2,1)}, bf16[8,6,128,128]{3,2,1,0:T(8,128)(2,1)S(1)}, u32[]{:S(2)}) copy-start(bf16[8,6,128,128]{3,2,1,0:T(8,128)(2,1)S(1)} %all_to_all.15.row_own) | copy-start | bytes 4718596
  136.7 14.9 %collective-permute-start.3 = (bf16[8,6,128,128]{3,2,1,0:T(8,128)(2,1)S(1)}, bf16[8,6,128,128]{3,2,1,0:T(8,128)(2,1)S(1)}, u32[]{:S(2)}, u32[]{:S(2)}) collective-permute-start(bf16[8,6,128,128]{3,2,1,0:T(8,128)(2,1)S(1)} %all_to_all.15.row_own), channel_id=1, source_target_pairs={{0,1},{1,0},{2,3},{3,2},{4,5},{5,4},{6,7},{7,6},{8,9},{9,8},{10,11... | collective-permute-start | bytes 4718600 | tf_op jit(solution)/shard_map/ppermute | solution.py:246
  136.7 38.6 %collective-permute-start.1 = (bf16[8,8,96,128]{3,2,1,0:T(8,128)(2,1)}, bf16[8,8,96,128]{3,2,1,0:T(8,128)(2,1)}, u32[]{:S(2)}, u32[]{:S(2)}) collective-permute-start(bf16[8,8,96,128]{3,2,1,0:T(8,128)(2,1)} %bitcast.31), channel_id=1, source_target_pairs={{0,16},{16,0},{32,48},{48,32},{64,80},{80,64},{96,112},{112,96},{1... | collective-permute-start | bytes 4718600 | tf_op jit(solution)/shard_map/ppermute | solution.py:219
  151.6 1.1 copy-start.1
Sparse Core Ops, SparseCore 0:
  19.4 60.3 all-gather.4
  97.1 42.3 all-gather.6

commit v3 on v2

--- a/solution.py
+++ b/solution.py
@@ -22,8 +22,8 @@
 
 
 SPREAD = [(q * N + j, spread_target(q, j) * N + q) for q in range(N) for j in range(N)]
-SPREAD_A = [(s, d) for s, d in SPREAD if s % N < 8]
-SPREAD_B = [(s - 8, d) for s, d in SPREAD if s % N >= 8]
+LOW_A = [(s, d) for s, d in SPREAD if s // N < 8]
+LOW_B = [(s, d + 8) for s, d in LOW_A]
 HALVE = [(n, n + 8) for n in range(8)]
 SWAP_CORE = [(c, c ^ 1) for c in range(N)]
 SAME_CORE = [[2 * i + k for i in range(8)] for k in (0, 1)]
@@ -51,53 +51,66 @@
     return lax.dot_general(left, right, (((0,), (0,)), ((), ())), preferred_element_type=F32)
 
 
-def panel_block_kernel(place, adj, base, own, faces, lower, upper, acc):
-    r, c = place[0], place[1]
+def panel_block_kernel(place, adj, base, own, faces, half, first, acc):
+    r, c = place[0], place[1]
+    n = c % 8
     acc[...] = base[...]
+
+    def add(a, value):
+        t = a - 4 * (c // 8)
+
+        @pl.when((t >= 0) & (t < 4))
+        def _():
+            acc[jnp.clip(t, 0, 3)] += value
+
+        @pl.when(a == 0)
+        def _():
+            acc[4] += value
+
     for g in range(4):
-        e = adj[c * 4 + g]
-
-        @pl.when((e % N == r) & (c < 8))
+        e = adj[n * 4 + g]
+
+        @pl.when(e % N == r)
         def _():
-            a = e // N
             right = right_of_chunks([faces[2 * (4 * (g % 2) + k) + g // 2] for k in range(4)])
-            acc[a] -= pair_product(left_of(own, (a, g ^ 1)), right)
-
-    @pl.when(r == c)
+            add(e // N, -pair_product(left_of(own, (e // N, g ^ 1)), right))
+
+    @pl.when(r == n)
     def _():
         for f in range(4):
-            acc[0] += pair_product(left_of(own, (0, f)), right_of(own, (0, f)))
-
-    lower[...] = acc[:4].astype(BF16)
-    upper[...] = acc[4:].astype(BF16)
-
-
-def couple(place, adj, own, faces, out, t, a, parity):
-    r, c = place[0], place[1]
-    for f in (0, 1) if parity == 0 else (2, 3):
-        n = adj[(a * N + r) * 4 + f]
-
-        @pl.when(n % N == c)
-        def _():
-            b = n // N
-            right = right_of_chunks([faces[4 * (1 - f % 2) + k, b] for k in range(4)])
-            rows = pl.ds(b, NB, stride=8)
-            out[t, rows, :] = out[t, rows, :] - pair_product(left_of(own, (t, f)), right)
-
-
-def assemble_kernel(place, adj, base, own, faces, out):
-    r, c = place[0], place[1]
-    a = pl.program_id(0)
+            add(jnp.int32(0), pair_product(left_of(own, (0, f)), right_of(own, (0, f))))
+
+    half[...] = acc[:4].astype(BF16)
+    first[...] = acc[4:].astype(BF16)
+
+
+def couple_kernel(place, adj, own, faces, out):
+    r, c = place[0], place[1]
+
+    def one_class(q, carry):
+        for h in range(2):
+            e = adj[((c // 2) * N + q) * 4 + 2 * (c % 2) + h]
+
+            @pl.when(e % N == r)
+            def _():
+                right = right_of(faces, (q // 2, (q % 2) ^ (r % 2), h))
+                out[q, h] = pair_product(left_of(own, (e // N, 2 * (c % 2) + 1 - h)), right).astype(BF16)
+
+        return carry
+
+    lax.fori_loop(0, N, one_class, 0)
+
+
+def assemble_kernel(place, base, own, out):
+    r, c = place[0], place[1]
     out[...] = base[...]
-    for parity in (0, 1):
-        pl.when(r % 2 == parity)(lambda: couple(place, adj, own, faces, out, 0, a, parity))
 
     @pl.when(r == c)
     def _():
         total = pair_product(left_of(own, (0, 0)), right_of(own, (0, 0)))
         for f in range(1, 4):
             total += pair_product(left_of(own, (0, f)), right_of(own, (0, f)))
-        rows = pl.ds(a, NB, stride=8)
+        rows = pl.ds(pl.program_id(0), NB, stride=8)
         out[0, rows, :] = out[0, rows, :] + total
 
 
@@ -150,7 +163,7 @@
 
 
 def update_kernel(
-    place, adj, readers, front, own, faces_x, w0r, w1r, cross, col_half, partner, diag, side, out, v0c, v1c,
+    place, adj, readers, front, couplings, w0r, w1r, cross, col_half, partner, diag, side, out, v0c, v1c,
 ):
     r, c = place[0], place[1]
     step = pl.program_id(0)
@@ -178,8 +191,14 @@
         for b in range(8):
             rows = pl.ds(b, NB, stride=8)
             out[t, rows, :] = front[t, rows, :] - change[t * NB : (t + 1) * NB, b * NB : (b + 1) * NB]
-        for parity in (0, 1):
-            pl.when(r % 2 != parity)(lambda: couple(place, adj, own, faces_x, out, t, 2 * step + t, parity))
+        for f in range(4):
+            n = adj[((2 * step + t) * N + r) * 4 + f]
+
+            @pl.when(n % N == c)
+            def _():
+                g = f ^ 1
+                rows = pl.ds(n // N, NB, stride=8)
+                out[t, rows, :] = out[t, rows, :] - couplings[2 * (n // N) + g // 2, g % 2].astype(F32)
 
 
 def pivot_tables(pivot_order, pivot_kind, inverse_diagonal, inverse_coupling):
@@ -212,40 +231,51 @@
     own = traces[:, 0]
     base = front_base.reshape(8, 8 * NB, NB)
 
+    mine = lax.dynamic_slice_in_dim(own.reshape(32, 3, NB, NB), 2 * c, 2, axis=0)
+    mine_x = lax.ppermute(mine, "row", SWAP_X)
+    faces = lax.all_gather(jnp.stack([mine, mine_x]), "row", axis=0, axis_index_groups=Z_LINES)
+
     chunk = (r // 2 + c // 2) % 8 + 8 * (c % 2)
-    piece = lax.dynamic_index_in_dim(own.reshape(8, N, 96, NB), chunk, 1, keepdims=False)
-    piece = lax.ppermute(piece, BOTH, SPREAD)
-    faces = lax.all_gather(piece, "row", axis=0, axis_index_groups=Z_LINES)
-    faces_x = lax.ppermute(faces, "row", SWAP_X)
-    low_faces = lax.all_to_all(jnp.broadcast_to(piece[:1], (N, 96, NB)), "row", 0, 0, tiled=True)
+    low = lax.dynamic_index_in_dim(own[0].reshape(N, 96, NB), chunk, 0, keepdims=False)
+    low_a = lax.ppermute(low, BOTH, LOW_A)
+    low_b = lax.ppermute(low, BOTH, LOW_B)
+    low = jnp.where(c < 8, low_a, low_b)
+    low_faces = lax.all_to_all(jnp.broadcast_to(low[None], (N, 96, NB)), "row", 0, 0, tiled=True)
 
     base_low = front_base[:, 0, :, 0, 0, :]
-    lower, upper = pl.pallas_call(
+    base_far = lax.ppermute(jnp.concatenate([base_low[4:], base_low[:1]]), "col", HALVE)
+    half, first = pl.pallas_call(
         panel_block_kernel,
-        out_shape=(jax.ShapeDtypeStruct((4, NB, NB), BF16),) * 2,
+        out_shape=(jax.ShapeDtypeStruct((4, NB, NB), BF16), jax.ShapeDtypeStruct((1, NB, NB), BF16)),
         in_specs=[smem(), smem(), vmem(), vmem(), vmem()],
         out_specs=(vmem(), vmem()),
-        scratch_shapes=[pltpu.VMEM((8, NB, NB), F32)],
+        scratch_shapes=[pltpu.VMEM((5, NB, NB), F32)],
         name="panel_block",
-    )(place, adj, base_low, own, low_faces)
-
-    spread_a = lax.ppermute(lower, BOTH, SPREAD_A)
-    spread_b = lax.ppermute(upper, BOTH, SPREAD_B)
-    spread = jnp.where((r // 2 - c // 2) % 8 < 4, spread_a, spread_b)
+    )(place, adj, jnp.where(c < 8, jnp.concatenate([base_low[:4], base_low[:1]]), base_far), own, low_faces)
+
+    spread = lax.ppermute(half, BOTH, SPREAD)
     other = lax.ppermute(spread, "row", SWAP_X)
-    pair = jnp.stack([spread, other])
+    pair, faces = lax.optimization_barrier((jnp.stack([spread, other]), faces))
     col_half = lax.all_gather(pair, "row", axis=0, axis_index_groups=Z_LINES)
 
-    cross_row = lax.all_to_all(jnp.broadcast_to(lower[:1], (N, NB, NB)), "row", 0, 0, tiled=True)[4:8]
-
-    moved = lax.ppermute(jnp.concatenate([upper, cross_row[2:]]), "col", HALVE)
-    half = jnp.where(c < 8, jnp.concatenate([lower, cross_row[:2]]), moved)
+    cross_row = lax.all_to_all(jnp.broadcast_to(first, (N, NB, NB)), "row", 0, 0, tiled=True)[4:8]
+
+    half = jnp.concatenate([half, jnp.where(c < 8, cross_row[:2], cross_row[2:])])
     row_own = lax.all_to_all(
         jnp.broadcast_to(half[None], (8,) + half.shape), "col", 0, 0, tiled=True, axis_index_groups=SAME_CORE
     )
     row_other = lax.ppermute(row_own, "col", SWAP_CORE)
 
     partner, diag, side = pivot_tables(pivot_order, pivot_kind, inverse_diagonal, inverse_coupling)
+
+    couplings = pl.pallas_call(
+        couple_kernel,
+        out_shape=jax.ShapeDtypeStruct((N, 2, NB, NB), BF16),
+        in_specs=[smem(), smem(), vmem(), vmem()],
+        out_specs=vmem(),
+        name="couple",
+    )(place, adj, own, faces)
+    couplings = lax.all_to_all(couplings, "col", 0, 0, tiled=True)
 
     front = pl.pallas_call(
         assemble_kernel,
@@ -253,14 +283,12 @@
         out_shape=jax.ShapeDtypeStruct((8, 8 * NB, NB), F32),
         in_specs=[
             smem(),
-            smem(),
             pl.BlockSpec((1, 8 * NB, NB), lambda a: (a, 0, 0)),
             pl.BlockSpec((1, 4, 3, NB, NB), lambda a: (a, 0, 0, 0, 0)),
-            vmem(),
         ],
         out_specs=pl.BlockSpec((1, 8 * NB, NB), lambda a: (a, 0, 0)),
         name="assemble",
-    )(place, adj, base, own, faces)
+    )(place, base, own)
 
     by_two = pl.BlockSpec((2 * NB, PW), lambda s: (s, 0))
     w0r, w1r, cross = pl.pallas_call(
@@ -282,7 +310,6 @@
             smem(),
             smem(),
             pl.BlockSpec((2, 8 * NB, NB), lambda s: (s, 0, 0)),
-            pl.BlockSpec((2, 4, 3, NB, NB), lambda s: (s, 0, 0, 0, 0)),
             vmem(),
             by_two,
             by_two,
@@ -295,7 +322,7 @@
         out_specs=pl.BlockSpec((2, 8 * NB, NB), lambda s: (s, 0, 0)),
         scratch_shapes=[pltpu.VMEM((8 * NB, PW), BF16), pltpu.VMEM((8 * NB, PW), BF16)],
         name="update",
-    )(place, adj, readers.reshape(-1), front, own, faces_x, w0r, w1r, cross, col_half, partner, diag, side)
+    )(place, adj, readers.reshape(-1), front, couplings, w0r, w1r, cross, col_half, partner, diag, side)
     return out.reshape(8, 1, NB, 8, 1, NB)
 
 

time: 196 us -> 181 us (0.923)
  waiting for transfers between devices: 55 us -> 38.7 us
  starting transfers between devices: 48.2 us -> 43.5 us
  blocking collectives: 29.6 us -> 33.7 us
  Pallas kernels: 28.4 us -> 31.7 us
  local copies, waits for them, and re-layouts: 14.2 us -> 11.6 us
    ppermute x5, waiting for transfers between devices: 35.3 us -> 24.8 us  [the longest x1 11.5 us: steps(): spread = lax.ppermute(half, BOTH, SPREAD)]
    pallas_call x0 -> x1, Pallas kernels: none -> 5.06 us  [steps(): pl.pallas_call(couple_kernel, out_shape=jax.ShapeDtypeStruct((N, 2, NB, N...]
    all_to_all x2 -> x3, waiting for transfers between devices: 15.5 us -> 10.5 us  [the longest x1 10.5 us: steps(): lax.all_to_all(jnp.broadcast_to(low[None], (N, 96, NB)), 'row', 0, 0, til...]
    all_to_all x1, blocking collectives: 29.6 us -> 33.7 us  [steps(): lax.all_to_all(jnp.broadcast_to(half[None], (8,) + half.shape), 'col', 0,...]
    all_to_all x2 -> x3, starting transfers between devices: 22.9 us -> 19.1 us  [the longest x1 9.88 us: steps(): lax.all_to_all(jnp.broadcast_to(low[None], (N, 96, NB)), 'row', 0, 0, til...]
  transfers between devices with their start and end apart: 11 -> 12, of which waited for: 6 -> 6; matrix products, arithmetic and copies ran while one was open for 8% -> 8% of each run, Pallas kernels for 9% -> 12%
where the time goes in v3:
time: 181 us; the launch traced here: 179 us
  starting transfers between devices  43.5 us (24%)
  waiting for transfers between devices  38.7 us (21%)
  blocking collectives  33.7 us (19%)
  Pallas kernels  31.7 us (18%)
  between operations  13.7 us (8%)
  local copies, waits for them, and re-layouts  11.6 us (6%)
  other arithmetic  5.98 us (3%)
    all_to_all x1, blocking collectives, steps(): lax.all_to_all(jnp.broadcast_to(half[None], (8,) + half.shape), 'col', 0,...  33.7 us
    ppermute x1, waiting for transfers between devices, steps(): spread = lax.ppermute(half, BOTH, SPREAD)  11.5 us
    all_to_all x1, waiting for transfers between devices, steps(): lax.all_to_all(jnp.broadcast_to(low[None], (N, 96, NB)), 'row', 0, 0, til...  10.5 us
    pallas_call x1, Pallas kernels, steps(): pl.pallas_call(update_kernel, grid=(4,), out_shape=jax.ShapeDtypeStruct((...  10.3 us
    all_to_all x1, starting transfers between devices, steps(): lax.all_to_all(jnp.broadcast_to(low[None], (N, 96, NB)), 'row', 0, 0, til...  9.88 us
    pallas_call x1, Pallas kernels, steps(): pl.pallas_call(assemble_kernel, grid=(8,), out_shape=jax.ShapeDtypeStruct...  7.35 us
    pallas_call x1, Pallas kernels, steps(): pl.pallas_call(row_side_kernel, grid=(4,), out_shape=(jax.ShapeDtypeStruc...  6.2 us
    ppermute x1, starting transfers between devices, steps(): low_b = lax.ppermute(low, BOTH, LOW_B)  6.19 us
  transfers between devices with their start and end apart: 12, of which 6 were waited for; matrix products, arithmetic and copies ran while one was open for 8% of the time, Pallas kernels for 12%

profile of v3, /device:TPU:8, one launch (start us, length us, event | category | flops | bytes accessed | tf_op | source)
XLA Modules:
  0.0 179.0 jit_solution(396723170647062629)
XLA Ops:
  6.5 0.9 constant_dynamic-slice_fusion
  7.5 3.1 %collective-permute-start.5 = (bf16[2,3,128,128]{3,2,1,0:T(8,128)(2,1)S(1)}, bf16[2,3,128,128]{3,2,1,0:T(8,128)(2,1)S(1)}, u32[]{:S(2)}, u32[]{:S(2)}) collective-permute-start(bf16[2,3,128,128]{3,2,1,0:T(8,128)(2,1)S(1)} %constant_dynamic-slice_fusion), channel_id=1, source_target_pairs={{0,16},{16,0},{32,48},{48,32},{64,80},{80,64},{96,112},{112,96},{1... | collective-permute-start | bytes 589832 | tf_op jit(solution)/shard_map/ppermute | solution.py:235
  10.6 0.9 fusion.3
  11.5 4.2 %collective-permute-done.5 = bf16[2,3,128,128]{3,2,1,0:T(8,128)(2,1)S(1)} collective-permute-done((bf16[2,3,128,128]{3,2,1,0:T(8,128)(2,1)S(1)}, bf16[2,3,128,128]{3,2,1,0:T(8,128)(2,1)S(1)}, u32[]{:S(2)}, u32[]{:S(2)}) %collective-permute-start.5) | collective-permute-done | bytes 196640 | tf_op jit(solution)/shard_map/ppermute | solution.py:235
  15.7 0.8 pad_maximum_fusion.2
  16.6 1.0 slice.45
  17.7 6.2 %collective-permute-start.2 = (bf16[96,128]{1,0:T(8,128)(2,1)S(1)}, bf16[96,128]{1,0:T(8,128)(2,1)S(1)}, u32[]{:S(2)}, u32[]{:S(2)}) collective-permute-start(bf16[96,128]{1,0:T(8,128)(2,1)S(1)} %dynamic-slice_bitcast_fusion), channel_id=1, source_target_pairs={{0,8},{1,24},{2,40},{3,56},{4,72},{5,88},{6,104},{7,120},{8,136},{... | collective-permute-start | bytes 73736 | tf_op jit(solution)/shard_map/ppermute | solution.py:241
  23.9 3.8 %collective-permute-start.1 = (bf16[96,128]{1,0:T(8,128)(2,1)S(1)}, bf16[96,128]{1,0:T(8,128)(2,1)S(1)}, u32[]{:S(2)}, u32[]{:S(2)}) collective-permute-start(bf16[96,128]{1,0:T(8,128)(2,1)S(1)} %dynamic-slice_bitcast_fusion), channel_id=1, source_target_pairs={{0,0},{1,16},{2,32},{3,48},{4,64},{5,80},{6,96},{7,112},{8,128},{9... | collective-permute-start | bytes 73736 | tf_op jit(solution)/shard_map/ppermute | solution.py:240
  27.7 5.3 %collective-permute-done.1 = bf16[96,128]{1,0:T(8,128)(2,1)S(1)} collective-permute-done((bf16[96,128]{1,0:T(8,128)(2,1)S(1)}, bf16[96,128]{1,0:T(8,128)(2,1)S(1)}, u32[]{:S(2)}, u32[]{:S(2)}) %collective-permute-start.1) | collective-permute-done | bytes 24608 | tf_op jit(solution)/shard_map/ppermute | solution.py:240
  33.0 0.8 broadcast_in_dim.65
  33.8 9.9 %all-to-all-start = ((bf16[16,96,128]{2,1,0:T(8,128)(2,1)}), bf16[16,96,128]{2,1,0:T(8,128)(2,1)S(1)}, u32[]{:S(2)}, u32[]{:S(2)}) async-start(bf16[16,96,128]{2,1,0:T(8,128)(2,1)} %broadcast_in_dim.65), calls=%async_computation | async-start | bytes 786432 | tf_op jit(solution)/shard_map/all_to_all | solution.py:243
  43.7 1.1 fusion.2
  44.8 0.8 slice.41
  45.6 2.3 %collective-permute-start = (f32[5,128,128]{2,1,0:T(8,128)S(1)}, f32[5,128,128]{2,1,0:T(8,128)S(1)}, u32[]{:S(2)}, u32[]{:S(2)}) collective-permute-start(f32[5,128,128]{2,1,0:T(8,128)S(1)} %pad_maximum_fusion), channel_id=1, source_target_pairs={{0,8},{1,9},{2,10},{3,11},{4,12},{5,13},{6,14},{7,15},{16,24},{17,... | collective-permute-start | bytes 983048 | tf_op jit(solution)/shard_map/ppermute | solution.py:246
  49.4 3.8 %collective-permute-done = f32[5,128,128]{2,1,0:T(8,128)S(1)} collective-permute-done((f32[5,128,128]{2,1,0:T(8,128)S(1)}, f32[5,128,128]{2,1,0:T(8,128)S(1)}, u32[]{:S(2)}, u32[]{:S(2)}) %collective-permute-start) | collective-permute-done | bytes 327712 | tf_op jit(solution)/shard_map/ppermute | solution.py:246
  54.0 10.5 %all-to-all-done.faces = bf16[16,96,128]{2,1,0:T(8,128)(2,1)S(1)} async-done(((bf16[16,96,128]{2,1,0:T(8,128)(2,1)}), bf16[16,96,128]{2,1,0:T(8,128)(2,1)S(1)}, u32[]{:S(2)}, u32[]{:S(2)}) %all-to-all-start) | async-done | bytes 393248 | tf_op jit(solution)/shard_map/all_to_all | solution.py:243
  65.2 2.8 %panel_block.1 = (bf16[4,128,128]{2,1,0:T(8,128)(2,1)}, bf16[1,128,128]{2,1,0:T(8,128)(2,1)}) custom-call(s32[2]{0:T(128)} %pad_add_fusion.place, s32[512]{0:T(512)} %reshape.31.adj, f32[5,128,128]{2,1,0:T(8,128)} %fusion.1.base, bf16[8,4,3,128,128]{4,3,2,1,0:T(8,128)(2,1)} %bitcast.31, bf16[16,96,128]{2,1,0:T(8,128)(2,1)} %copy-done.2), custom_call_target="tpu_custom_call" | custom-call | tf_op jit(solution)/shard_map/panel_block/pallas_call | solution.py:247
  68.1 1.7 broadcast_in_dim.67
  69.7 3.6 %all-to-all-start.2 = ((bf16[16,128,128]{2,1,0:T(8,128)(2,1)}), bf16[16,128,128]{2,1,0:T(8,128)(2,1)S(1)}, u32[]{:S(2)}, u32[]{:S(2)}) async-start(bf16[16,128,128]{2,1,0:T(8,128)(2,1)} %broadcast_in_dim.67), calls=%async_computation.2 | async-start | bytes 1048576 | tf_op jit(solution)/shard_map/all_to_all | solution.py:261
  73.4 5.8 %collective-permute-start.3 = (bf16[4,128,128]{2,1,0:T(8,128)(2,1)}, bf16[4,128,128]{2,1,0:T(8,128)(2,1)S(1)}, u32[]{:S(2)}, u32[]{:S(2)}) collective-permute-start(bf16[4,128,128]{2,1,0:T(8,128)(2,1)} %get-tuple-element.12), channel_id=1, source_target_pairs={{0,0},{1,16},{2,32},{3,48},{4,64},{5,80},{6,96},{7,112},{8,128},{9... | collective-permute-start | bytes 393224 | tf_op jit(solution)/shard_map/ppermute | solution.py:256
  79.2 11.5 %collective-permute-done.3 = bf16[4,128,128]{2,1,0:T(8,128)(2,1)S(1)} collective-permute-done((bf16[4,128,128]{2,1,0:T(8,128)(2,1)}, bf16[4,128,128]{2,1,0:T(8,128)(2,1)S(1)}, u32[]{:S(2)}, u32[]{:S(2)}) %collective-permute-start.3) | collective-permute-done | bytes 131104 | tf_op jit(solution)/shard_map/ppermute | solution.py:256
  90.6 3.1 %collective-permute-start.4 = (bf16[4,128,128]{2,1,0:T(8,128)(2,1)S(1)}, bf16[4,128,128]{2,1,0:T(8,128)(2,1)S(1)}, u32[]{:S(2)}, u32[]{:S(2)}) collective-permute-start(bf16[4,128,128]{2,1,0:T(8,128)(2,1)S(1)} %collective-permute-done.3), channel_id=1, source_target_pairs={{0,16},{16,0},{32,48},{48,32},{64,80},{80,64},{96,112},{112,96},{1... | collective-permute-start | bytes 393224 | tf_op jit(solution)/shard_map/ppermute | solution.py:257
  93.8 3.3 %collective-permute-done.4 = bf16[4,128,128]{2,1,0:T(8,128)(2,1)S(1)} collective-permute-done((bf16[4,128,128]{2,1,0:T(8,128)(2,1)S(1)}, bf16[4,128,128]{2,1,0:T(8,128)(2,1)S(1)}, u32[]{:S(2)}, u32[]{:S(2)}) %collective-permute-start.4) | collective-permute-done | bytes 131104 | tf_op jit(solution)/shard_map/ppermute | solution.py:257
  98.3 33.7 %all_to_all.20.row_own = bf16[8,6,128,128]{3,2,1,0:T(8,128)(2,1)S(1)} all-to-all(bf16[8,6,128,128]{3,2,1,0:T(8,128)(2,1)S(1)} %broadcast_in_dim.68), channel_id=1, replica_groups={{0,2,4,6,8,10,12,14},{1,3,5,7,9,11,13,15},{16,18,20,22,24,26,28,30},{17..., dimensions={0} | all-to-all | bytes 3145728 | tf_op jit(solution)/shard_map/all_to_all | solution.py:264
  132.1 5.1 %couple.1 = bf16[16,2,128,128]{3,2,1,0:T(8,128)(2,1)} custom-call(s32[2]{0:T(128)} %pad_add_fusion.place, s32[512]{0:T(512)} %reshape.31.adj, bf16[8,4,3,128,128]{4,3,2,1,0:T(8,128)(2,1)} %bitcast.32, bf16[8,2,2,3,128,128]{5,4,3,2,1,0:T(8,128)(2,1)} %bitcast.35), custom_call_target="tpu_custom_call" | custom-call | tf_op jit(solution)/shard_map/couple/pallas_call | solution.py:271
  137.1 5.7 %all-to-all-start.1 = ((bf16[16,2,128,128]{3,2,1,0:T(8,128)(2,1)}), bf16[16,2,128,128]{3,2,1,0:T(8,128)(2,1)S(1)}, u32[]{:S(2)}, u32[]{:S(2)}) async-start(bf16[16,2,128,128]{3,2,1,0:T(8,128)(2,1)} %couple.1), calls=%async_computation.1 | async-start | bytes 2097152 | tf_op jit(solution)/shard_map/all_to_all | solution.py:278
  144.3 7.3 %assemble.1.front = f32[8,1024,128]{2,1,0:T(8,128)} custom-call(s32[2]{0:T(128)} %pad_add_fusion.place, f32[8,1024,128]{2,1,0:T(8,128)} %bitcast.34, bf16[8,4,3,128,128]{4,3,2,1,0:T(8,128)(2,1)} %bitcast.33), custom_call_target="tpu_custom_call" | custom-call | tf_op jit(solution)/shard_map/assemble/pallas_call | solution.py:280
  152.1 1.2 select_reduce_fusion
  153.3 1.4 fusion.partner
  154.7 6.2 %row_side.1 = (bf16[1024,512]{1,0:T(8,128)(2,1)}, bf16[1024,512]{1,0:T(8,128)(2,1)}, bf16[512,512]{1,0:T(8,128)(2,1)}) custom-call(s32[2]{0:T(128)} %pad_add_fusion.place, s32[256]{0:T(256)} %bitcast.46, bf16[8,6,128,128]{3,2,1,0:T(8,128)(2,1)} %copy-done, bf16[8,6,128,128]{3,2,1,0:T(8,128)(2,1)} %collective-permute-done.6.row_other, ...), custom_call_target="tpu_custom_call" | custom-call | tf_op jit(solution)/shard_map/row_side/pallas_call | solution.py:294
  160.9 0.9 copy-done.1
  161.9 10.3 %update.1 = f32[8,1024,128]{2,1,0:T(8,128)} custom-call(s32[2]{0:T(128)} %pad_add_fusion.place, s32[512]{0:T(512)} %reshape.31.adj, s32[256]{0:T(256)} %bitcast.47, f32[8,1024,128]{2,1,0:T(8,128)} %assemble.1.front, bf16[16,2,128,128]{3,2,1,0:T(8,128)(2,1)} %copy-done.1, bf16[1024,512]{1,0:T(8,128)(2,1)} %get-tuple-element.15.w0r, ...), custom_call_target="tpu_custom_call" | custom-call | tf_op jit(solution)/shard_map/update/pallas_call | solution.py:304
  (48 shorter events, 6.1 us)
Async XLA Ops:
  6.5 91.3 %all-gather.5.cloned.1.call-start = ((), (), s32[]{:S(2)}) async-start(), calls=%async_computation.4 | async-start | bytes 3538944 | tf_op jit(solution)/shard_map/all_gather | solution.py:236
  7.5 8.2 %collective-permute-start.5 = (bf16[2,3,128,128]{3,2,1,0:T(8,128)(2,1)S(1)}, bf16[2,3,128,128]{3,2,1,0:T(8,128)(2,1)S(1)}, u32[]{:S(2)}, u32[]{:S(2)}) collective-permute-start(bf16[2,3,128,128]{3,2,1,0:T(8,128)(2,1)S(1)} %constant_dynamic-slice_fusion), channel_id=1, source_target_pairs={{0,16},{16,0},{32,48},{48,32},{64,80},{80,64},{96,112},{112,96},{1... | collective-permute-start | bytes 589832 | tf_op jit(solution)/shard_map/ppermute | solution.py:235
  16.5 31.4 %copy-start.8 = (s32[128,4]{0,1:T(4,128)S(1)}, s32[128,4]{0,1:T(4,128)}, u32[]{:S(2)}) copy-start(s32[128,4]{0,1:T(4,128)} %param.10) | copy-start | bytes 6148
  17.7 10.0 %collective-permute-start.2 = (bf16[96,128]{1,0:T(8,128)(2,1)S(1)}, bf16[96,128]{1,0:T(8,128)(2,1)S(1)}, u32[]{:S(2)}, u32[]{:S(2)}) collective-permute-start(bf16[96,128]{1,0:T(8,128)(2,1)S(1)} %dynamic-slice_bitcast_fusion), channel_id=1, source_target_pairs={{0,8},{1,24},{2,40},{3,56},{4,72},{5,88},{6,104},{7,120},{8,136},{... | collective-permute-start | bytes 73736 | tf_op jit(solution)/shard_map/ppermute | solution.py:241
  23.9 9.1 %collective-permute-start.1 = (bf16[96,128]{1,0:T(8,128)(2,1)S(1)}, bf16[96,128]{1,0:T(8,128)(2,1)S(1)}, u32[]{:S(2)}, u32[]{:S(2)}) collective-permute-start(bf16[96,128]{1,0:T(8,128)(2,1)S(1)} %dynamic-slice_bitcast_fusion), channel_id=1, source_target_pairs={{0,0},{1,16},{2,32},{3,48},{4,64},{5,80},{6,96},{7,112},{8,128},{9... | collective-permute-start | bytes 73736 | tf_op jit(solution)/shard_map/ppermute | solution.py:240
  33.8 30.7 %all-to-all-start = ((bf16[16,96,128]{2,1,0:T(8,128)(2,1)}), bf16[16,96,128]{2,1,0:T(8,128)(2,1)S(1)}, u32[]{:S(2)}, u32[]{:S(2)}) async-start(bf16[16,96,128]{2,1,0:T(8,128)(2,1)} %broadcast_in_dim.65), calls=%async_computation | async-start | bytes 786432 | tf_op jit(solution)/shard_map/all_to_all | solution.py:243
  45.6 7.5 %collective-permute-start = (f32[5,128,128]{2,1,0:T(8,128)S(1)}, f32[5,128,128]{2,1,0:T(8,128)S(1)}, u32[]{:S(2)}, u32[]{:S(2)}) collective-permute-start(f32[5,128,128]{2,1,0:T(8,128)S(1)} %pad_maximum_fusion), channel_id=1, source_target_pairs={{0,8},{1,9},{2,10},{3,11},{4,12},{5,13},{6,14},{7,15},{16,24},{17,... | collective-permute-start | bytes 983048 | tf_op jit(solution)/shard_map/ppermute | solution.py:246
  64.5 0.7 copy-start.2
  68.1 29.9 %copy-start.3 = (bf16[4,128,128]{2,1,0:T(8,128)(2,1)S(1)}, bf16[4,128,128]{2,1,0:T(8,128)(2,1)}, u32[]{:S(2)}) copy-start(bf16[4,128,128]{2,1,0:T(8,128)(2,1)} %get-tuple-element.12) | copy-start | bytes 393220
  69.7 28.1 %all-to-all-start.2 = ((bf16[16,128,128]{2,1,0:T(8,128)(2,1)}), bf16[16,128,128]{2,1,0:T(8,128)(2,1)S(1)}, u32[]{:S(2)}, u32[]{:S(2)}) async-start(bf16[16,128,128]{2,1,0:T(8,128)(2,1)} %broadcast_in_dim.67), calls=%async_computation.2 | async-start | bytes 1048576 | tf_op jit(solution)/shard_map/all_to_all | solution.py:261
  73.3 87.6 %all-gather.7.cloned.1.call-start = ((), (), s32[]{:S(2)}) async-start(), calls=%async_computation.5 | async-start | bytes 2359296 | tf_op jit(solution)/shard_map/all_gather | solution.py:259
  73.4 17.3 %collective-permute-start.3 = (bf16[4,128,128]{2,1,0:T(8,128)(2,1)}, bf16[4,128,128]{2,1,0:T(8,128)(2,1)S(1)}, u32[]{:S(2)}, u32[]{:S(2)}) collective-permute-start(bf16[4,128,128]{2,1,0:T(8,128)(2,1)} %get-tuple-element.12), channel_id=1, source_target_pairs={{0,0},{1,16},{2,32},{3,48},{4,64},{5,80},{6,96},{7,112},{8,128},{9... | collective-permute-start | bytes 393224 | tf_op jit(solution)/shard_map/ppermute | solution.py:256
  90.6 6.5 %collective-permute-start.4 = (bf16[4,128,128]{2,1,0:T(8,128)(2,1)S(1)}, bf16[4,128,128]{2,1,0:T(8,128)(2,1)S(1)}, u32[]{:S(2)}, u32[]{:S(2)}) collective-permute-start(bf16[4,128,128]{2,1,0:T(8,128)(2,1)S(1)} %collective-permute-done.3), channel_id=1, source_target_pairs={{0,16},{16,0},{32,48},{48,32},{64,80},{80,64},{96,112},{112,96},{1... | collective-permute-start | bytes 393224 | tf_op jit(solution)/shard_map/ppermute | solution.py:257
  132.1 5.1 %copy-start = (bf16[8,6,128,128]{3,2,1,0:T(8,128)(2,1)}, bf16[8,6,128,128]{3,2,1,0:T(8,128)(2,1)S(1)}, u32[]{:S(2)}) copy-start(bf16[8,6,128,128]{3,2,1,0:T(8,128)(2,1)S(1)} %all_to_all.20.row_own) | copy-start | bytes 4718596
  132.1 22.6 %collective-permute-start.6 = (bf16[8,6,128,128]{3,2,1,0:T(8,128)(2,1)S(1)}, bf16[8,6,128,128]{3,2,1,0:T(8,128)(2,1)}, u32[]{:S(2)}, u32[]{:S(2)}) collective-permute-start(bf16[8,6,128,128]{3,2,1,0:T(8,128)(2,1)S(1)} %all_to_all.20.row_own), channel_id=1, source_target_pairs={{0,1},{1,0},{2,3},{3,2},{4,5},{5,4},{6,7},{7,6},{8,9},{9,8},{10,11... | collective-permute-start | bytes 4718600 | tf_op jit(solution)/shard_map/ppermute | solution.py:267
  137.1 5.7 %copy-start.5 = (f32[2,512]{1,0:T(2,128)S(1)}, f32[2,512]{1,0:T(2,128)}, u32[]{:S(2)}) copy-start(f32[2,512]{1,0:T(2,128)} %param.14) | copy-start | bytes 12292
  137.1 5.7 %copy-start.6 = (s32[2,512]{1,0:T(2,128)S(1)}, s32[2,512]{1,0:T(2,128)}, u32[]{:S(2)}) copy-start(s32[2,512]{1,0:T(2,128)} %param.12) | copy-start | bytes 12292
  137.1 6.4 %copy-start.4 = (s32[2,512]{1,0:T(2,128)S(1)}, s32[2,512]{1,0:T(2,128)}, u32[]{:S(2)}) copy-start(s32[2,512]{1,0:T(2,128)} %param.11) | copy-start | bytes 12292
  137.1 23.7 %all-to-all-start.1 = ((bf16[16,2,128,128]{3,2,1,0:T(8,128)(2,1)}), bf16[16,2,128,128]{3,2,1,0:T(8,128)(2,1)S(1)}, u32[]{:S(2)}, u32[]{:S(2)}) async-start(bf16[16,2,128,128]{3,2,1,0:T(8,128)(2,1)} %couple.1), calls=%async_computation.1 | async-start | bytes 2097152 | tf_op jit(solution)/shard_map/all_to_all | solution.py:278
  144.3 7.8 %copy-start.7 = (f32[2,512]{1,0:T(2,128)S(1)}, f32[2,512]{1,0:T(2,128)}, u32[]{:S(2)}) copy-start(f32[2,512]{1,0:T(2,128)} %param.13) | copy-start | bytes 12292
  160.9 1.0 copy-start.1
Sparse Core Ops, SparseCore 0:
  16.7 56.2 all-gather.4
  98.0 44.4 all-gather.6

commit v4 on v3

--- a/solution.py
+++ b/solution.py
@@ -81,7 +81,7 @@
             add(jnp.int32(0), pair_product(left_of(own, (0, f)), right_of(own, (0, f))))
 
     half[...] = acc[:4].astype(BF16)
-    first[...] = acc[4:].astype(BF16)
+    first[0] = acc[4, pl.ds(pl.multiple_of((NB // 2) * (c // 8), NB // 2), NB // 2), :].astype(BF16)
 
 
 def couple_kernel(place, adj, own, faces, out):
@@ -140,8 +140,10 @@
         for i in range(4):
             kept = keep(readers, 0, 4 + i)
             for n in range(4):
-                tile = tile_of(n, i // 2, 4 + i % 2).astype(F32) * kept
-                cross[i * NB : (i + 1) * NB, n * NB : (n + 1) * NB] = tile.astype(BF16)
+                for h in range(2):
+                    tile = tile_of(n, h, 4 + i // 2)[(i % 2) * (NB // 2) : (i % 2 + 1) * (NB // 2)].astype(F32) * kept
+                    top = i * NB + h * (NB // 2)
+                    cross[top : top + NB // 2, n * NB : (n + 1) * NB] = tile.astype(BF16)
 
     for t in range(2):
         a = 2 * step + t
@@ -187,12 +189,12 @@
             v1c[b * NB : (b + 1) * NB, :] = (fresh[b * NB : (b + 1) * NB] * kept).astype(BF16)
 
     change = dot_nt(w0r[...], v0c[...]) + dot_nt(w1r[...], v1c[...])
-    for t in range(2):
+    for t in range(4):
         for b in range(8):
             rows = pl.ds(b, NB, stride=8)
             out[t, rows, :] = front[t, rows, :] - change[t * NB : (t + 1) * NB, b * NB : (b + 1) * NB]
         for f in range(4):
-            n = adj[((2 * step + t) * N + r) * 4 + f]
+            n = adj[((4 * step + t) * N + r) * 4 + f]
 
             @pl.when(n % N == c)
             def _():
@@ -246,7 +248,7 @@
     base_far = lax.ppermute(jnp.concatenate([base_low[4:], base_low[:1]]), "col", HALVE)
     half, first = pl.pallas_call(
         panel_block_kernel,
-        out_shape=(jax.ShapeDtypeStruct((4, NB, NB), BF16), jax.ShapeDtypeStruct((1, NB, NB), BF16)),
+        out_shape=(jax.ShapeDtypeStruct((4, NB, NB), BF16), jax.ShapeDtypeStruct((1, NB // 2, NB), BF16)),
         in_specs=[smem(), smem(), vmem(), vmem(), vmem()],
         out_specs=(vmem(), vmem()),
         scratch_shapes=[pltpu.VMEM((5, NB, NB), F32)],
@@ -255,12 +257,12 @@
 
     spread = lax.ppermute(half, BOTH, SPREAD)
     other = lax.ppermute(spread, "row", SWAP_X)
-    pair, faces = lax.optimization_barrier((jnp.stack([spread, other]), faces))
+    pair = jnp.stack([spread, other])
     col_half = lax.all_gather(pair, "row", axis=0, axis_index_groups=Z_LINES)
 
-    cross_row = lax.all_to_all(jnp.broadcast_to(first, (N, NB, NB)), "row", 0, 0, tiled=True)[4:8]
-
-    half = jnp.concatenate([half, jnp.where(c < 8, cross_row[:2], cross_row[2:])])
+    cross_row = lax.all_to_all(jnp.broadcast_to(first, (N, NB // 2, NB)), "row", 0, 0, tiled=True)[4:8]
+
+    half = jnp.concatenate([half, cross_row.reshape(2, NB, NB)])
     row_own = lax.all_to_all(
         jnp.broadcast_to(half[None], (8,) + half.shape), "col", 0, 0, tiled=True, axis_index_groups=SAME_CORE
     )
@@ -303,23 +305,23 @@
 
     out = pl.pallas_call(
         update_kernel,
-        grid=(4,),
+        grid=(2,),
         out_shape=jax.ShapeDtypeStruct((8, 8 * NB, NB), F32),
         in_specs=[
             smem(),
             smem(),
             smem(),
-            pl.BlockSpec((2, 8 * NB, NB), lambda s: (s, 0, 0)),
-            vmem(),
-            by_two,
-            by_two,
+            pl.BlockSpec((4, 8 * NB, NB), lambda s: (s, 0, 0)),
+            vmem(),
+            pl.BlockSpec((4 * NB, PW), lambda s: (s, 0)),
+            pl.BlockSpec((4 * NB, PW), lambda s: (s, 0)),
             vmem(),
             vmem(),
             vmem(),
             vmem(),
             vmem(),
         ],
-        out_specs=pl.BlockSpec((2, 8 * NB, NB), lambda s: (s, 0, 0)),
+        out_specs=pl.BlockSpec((4, 8 * NB, NB), lambda s: (s, 0, 0)),
         scratch_shapes=[pltpu.VMEM((8 * NB, PW), BF16), pltpu.VMEM((8 * NB, PW), BF16)],
         name="update",
     )(place, adj, readers.reshape(-1), front, couplings, w0r, w1r, cross, col_half, partner, diag, side)

time: 181 us -> 181 us (level)
  starting transfers between devices: 43.5 us -> 36 us
  blocking collectives: 33.7 us -> 41.1 us
    all_to_all x0 -> x1, blocking collectives: none -> 19.5 us  [steps(): lax.all_to_all(jnp.broadcast_to(first, (N, NB // 2, NB)), 'row', 0, 0, ti...]
    all_to_all x1, blocking collectives: 33.7 us -> 21.6 us  [steps(): lax.all_to_all(jnp.broadcast_to(half[None], (8,) + half.shape), 'col', 0,...]
    all_to_all x1 -> x0, starting transfers between devices: 3.57 us -> none  [steps(): lax.all_to_all(jnp.broadcast_to(first, (N, NB, NB)), 'row', 0, 0, tiled=T...]
    ppermute x1, starting transfers between devices: 5.77 us -> 2.54 us  [steps(): spread = lax.ppermute(half, BOTH, SPREAD)]
  transfers between devices with their start and end apart: 12 -> 11, of which waited for: 6 -> 6; matrix products, arithmetic and copies ran while one was open for 8% -> 8% of each run, Pallas kernels for 12% -> 12%
where the time goes in v4:
time: 181 us; the launch traced here: 180 us
  blocking collectives  41.1 us (23%)
  waiting for transfers between devices  39.6 us (22%)
  starting transfers between devices  36 us (20%)
  Pallas kernels  31.6 us (17%)
  between operations  13.7 us (8%)
  local copies, waits for them, and re-layouts  10.8 us (6%)
  other arithmetic  6.91 us (4%)
    all_to_all x1, blocking collectives, steps(): lax.all_to_all(jnp.broadcast_to(half[None], (8,) + half.shape), 'col', 0,...  21.6 us
    all_to_all x1, blocking collectives, steps(): lax.all_to_all(jnp.broadcast_to(first, (N, NB // 2, NB)), 'row', 0, 0, ti...  19.5 us
    ppermute x1, waiting for transfers between devices, steps(): spread = lax.ppermute(half, BOTH, SPREAD)  11 us
    all_to_all x1, waiting for transfers between devices, steps(): lax.all_to_all(jnp.broadcast_to(low[None], (N, 96, NB)), 'row', 0, 0, til...  10.5 us
    pallas_call x1, Pallas kernels, steps(): pl.pallas_call(update_kernel, grid=(2,), out_shape=jax.ShapeDtypeStruct((...  10.2 us
    all_to_all x1, starting transfers between devices, steps(): lax.all_to_all(jnp.broadcast_to(low[None], (N, 96, NB)), 'row', 0, 0, til...  9.88 us
    pallas_call x1, Pallas kernels, steps(): pl.pallas_call(assemble_kernel, grid=(8,), out_shape=jax.ShapeDtypeStruct...  7.38 us
    ppermute x1, starting transfers between devices, steps(): low_b = lax.ppermute(low, BOTH, LOW_B)  6.19 us
  transfers between devices with their start and end apart: 11, of which 6 were waited for; matrix products, arithmetic and copies ran while one was open for 8% of the time, Pallas kernels for 12%

profile of v4, /device:TPU:8, one launch (start us, length us, event | category | flops | bytes accessed | tf_op | source)
XLA Modules:
  0.0 179.6 jit_solution(7088210470832114159)
XLA Ops:
  6.5 0.9 constant_dynamic-slice_fusion
  7.5 3.1 %collective-permute-start = (bf16[2,3,128,128]{3,2,1,0:T(8,128)(2,1)S(1)}, bf16[2,3,128,128]{3,2,1,0:T(8,128)(2,1)S(1)}, u32[]{:S(2)}, u32[]{:S(2)}) collective-permute-start(bf16[2,3,128,128]{3,2,1,0:T(8,128)(2,1)S(1)} %constant_dynamic-slice_fusion), channel_id=1, source_target_pairs={{0,16},{16,0},{32,48},{48,32},{64,80},{80,64},{96,112},{112,96},{1... | collective-permute-start | bytes 589832 | tf_op jit(solution)/shard_map/ppermute | solution.py:237
  10.6 0.9 fusion.3
  11.5 4.2 %collective-permute-done = bf16[2,3,128,128]{3,2,1,0:T(8,128)(2,1)S(1)} collective-permute-done((bf16[2,3,128,128]{3,2,1,0:T(8,128)(2,1)S(1)}, bf16[2,3,128,128]{3,2,1,0:T(8,128)(2,1)S(1)}, u32[]{:S(2)}, u32[]{:S(2)}) %collective-permute-start) | collective-permute-done | bytes 196640 | tf_op jit(solution)/shard_map/ppermute | solution.py:237
  15.7 0.8 pad_maximum_fusion.2
  16.6 1.0 slice.39
  17.7 6.2 %collective-permute-start.3 = (bf16[96,128]{1,0:T(8,128)(2,1)S(1)}, bf16[96,128]{1,0:T(8,128)(2,1)S(1)}, u32[]{:S(2)}, u32[]{:S(2)}) collective-permute-start(bf16[96,128]{1,0:T(8,128)(2,1)S(1)} %dynamic-slice_bitcast_fusion), channel_id=1, source_target_pairs={{0,8},{1,24},{2,40},{3,56},{4,72},{5,88},{6,104},{7,120},{8,136},{... | collective-permute-start | bytes 73736 | tf_op jit(solution)/shard_map/ppermute | solution.py:243
  23.8 3.8 %collective-permute-start.2 = (bf16[96,128]{1,0:T(8,128)(2,1)S(1)}, bf16[96,128]{1,0:T(8,128)(2,1)S(1)}, u32[]{:S(2)}, u32[]{:S(2)}) collective-permute-start(bf16[96,128]{1,0:T(8,128)(2,1)S(1)} %dynamic-slice_bitcast_fusion), channel_id=1, source_target_pairs={{0,0},{1,16},{2,32},{3,48},{4,64},{5,80},{6,96},{7,112},{8,128},{9... | collective-permute-start | bytes 73736 | tf_op jit(solution)/shard_map/ppermute | solution.py:242
  27.7 5.3 %collective-permute-done.2 = bf16[96,128]{1,0:T(8,128)(2,1)S(1)} collective-permute-done((bf16[96,128]{1,0:T(8,128)(2,1)S(1)}, bf16[96,128]{1,0:T(8,128)(2,1)S(1)}, u32[]{:S(2)}, u32[]{:S(2)}) %collective-permute-start.2) | collective-permute-done | bytes 24608 | tf_op jit(solution)/shard_map/ppermute | solution.py:242
  33.0 0.8 broadcast_in_dim.65
  33.8 9.9 %all-to-all-start.1 = ((bf16[16,96,128]{2,1,0:T(8,128)(2,1)}), bf16[16,96,128]{2,1,0:T(8,128)(2,1)S(1)}, u32[]{:S(2)}, u32[]{:S(2)}) async-start(bf16[16,96,128]{2,1,0:T(8,128)(2,1)} %broadcast_in_dim.65), calls=%async_computation.1 | async-start | bytes 786432 | tf_op jit(solution)/shard_map/all_to_all | solution.py:245
  43.7 1.1 fusion.2
  44.8 0.8 slice.35
  45.7 2.3 %collective-permute-start.1 = (f32[5,128,128]{2,1,0:T(8,128)S(1)}, f32[5,128,128]{2,1,0:T(8,128)S(1)}, u32[]{:S(2)}, u32[]{:S(2)}) collective-permute-start(f32[5,128,128]{2,1,0:T(8,128)S(1)} %pad_maximum_fusion), channel_id=1, source_target_pairs={{0,8},{1,9},{2,10},{3,11},{4,12},{5,13},{6,14},{7,15},{16,24},{17,... | collective-permute-start | bytes 983048 | tf_op jit(solution)/shard_map/ppermute | solution.py:248
  49.5 3.7 %collective-permute-done.1 = f32[5,128,128]{2,1,0:T(8,128)S(1)} collective-permute-done((f32[5,128,128]{2,1,0:T(8,128)S(1)}, f32[5,128,128]{2,1,0:T(8,128)S(1)}, u32[]{:S(2)}, u32[]{:S(2)}) %collective-permute-start.1) | collective-permute-done | bytes 327712 | tf_op jit(solution)/shard_map/ppermute | solution.py:248
  54.0 10.5 %all-to-all-done.1.faces = bf16[16,96,128]{2,1,0:T(8,128)(2,1)S(1)} async-done(((bf16[16,96,128]{2,1,0:T(8,128)(2,1)}), bf16[16,96,128]{2,1,0:T(8,128)(2,1)S(1)}, u32[]{:S(2)}, u32[]{:S(2)}) %all-to-all-start.1) | async-done | bytes 393248 | tf_op jit(solution)/shard_map/all_to_all | solution.py:245
  65.2 2.8 %panel_block.1 = (bf16[4,128,128]{2,1,0:T(8,128)(2,1)}, bf16[1,64,128]{2,1,0:T(8,128)(2,1)}) custom-call(s32[2]{0:T(128)} %pad_add_fusion.place, s32[512]{0:T(512)} %reshape.34.adj, f32[5,128,128]{2,1,0:T(8,128)} %fusion.1.base, bf16[8,4,3,128,128]{4,3,2,1,0:T(8,128)(2,1)} %bitcast.32, bf16[16,96,128]{2,1,0:T(8,128)(2,1)} %copy-done.2), custom_call_target="tpu_custom_call" | custom-call | tf_op jit(solution)/shard_map/panel_block/pallas_call | solution.py:249
  68.0 2.5 %collective-permute-start.5 = (bf16[4,128,128]{2,1,0:T(8,128)(2,1)}, bf16[4,128,128]{2,1,0:T(8,128)(2,1)S(1)}, u32[]{:S(2)}, u32[]{:S(2)}) collective-permute-start(bf16[4,128,128]{2,1,0:T(8,128)(2,1)} %get-tuple-element.10), channel_id=1, source_target_pairs={{0,0},{1,16},{2,32},{3,48},{4,64},{5,80},{6,96},{7,112},{8,128},{9... | collective-permute-start | bytes 393224 | tf_op jit(solution)/shard_map/ppermute | solution.py:258
  70.6 11.0 %collective-permute-done.5 = bf16[4,128,128]{2,1,0:T(8,128)(2,1)S(1)} collective-permute-done((bf16[4,128,128]{2,1,0:T(8,128)(2,1)}, bf16[4,128,128]{2,1,0:T(8,128)(2,1)S(1)}, u32[]{:S(2)}, u32[]{:S(2)}) %collective-permute-start.5) | collective-permute-done | bytes 131104 | tf_op jit(solution)/shard_map/ppermute | solution.py:258
  81.5 2.6 %collective-permute-start.6 = (bf16[4,128,128]{2,1,0:T(8,128)(2,1)S(1)}, bf16[4,128,128]{2,1,0:T(8,128)(2,1)S(1)}, u32[]{:S(2)}, u32[]{:S(2)}) collective-permute-start(bf16[4,128,128]{2,1,0:T(8,128)(2,1)S(1)} %collective-permute-done.5), channel_id=1, source_target_pairs={{0,16},{16,0},{32,48},{48,32},{64,80},{80,64},{96,112},{112,96},{1... | collective-permute-start | bytes 393224 | tf_op jit(solution)/shard_map/ppermute | solution.py:259
  84.2 4.9 %collective-permute-done.6 = bf16[4,128,128]{2,1,0:T(8,128)(2,1)S(1)} collective-permute-done((bf16[4,128,128]{2,1,0:T(8,128)(2,1)S(1)}, bf16[4,128,128]{2,1,0:T(8,128)(2,1)S(1)}, u32[]{:S(2)}, u32[]{:S(2)}) %collective-permute-start.6) | collective-permute-done | bytes 131104 | tf_op jit(solution)/shard_map/ppermute | solution.py:259
  90.6 19.5 %all_to_all.20 = bf16[16,64,128]{2,1,0:T(8,128)(2,1)S(1)} all-to-all(bf16[16,64,128]{2,1,0:T(8,128)(2,1)S(1)} %broadcast_in_dim.67), channel_id=1, replica_groups=mesh['row'=16,'col'=16] {'row'}, dimensions={0} | all-to-all | bytes 524288 | tf_op jit(solution)/shard_map/all_to_all | solution.py:263
  110.1 0.9 pad_maximum_fusion.4
  111.4 21.6 %all_to_all.21.row_own = bf16[8,6,128,128]{3,2,1,0:T(8,128)(2,1)S(1)} all-to-all(bf16[8,6,128,128]{3,2,1,0:T(8,128)(2,1)S(1)} %broadcast_in_dim.68), channel_id=1, replica_groups={{0,2,4,6,8,10,12,14},{1,3,5,7,9,11,13,15},{16,18,20,22,24,26,28,30},{17..., dimensions={0} | all-to-all | bytes 3145728 | tf_op jit(solution)/shard_map/all_to_all | solution.py:266
  133.0 5.0 %couple.1 = bf16[16,2,128,128]{3,2,1,0:T(8,128)(2,1)} custom-call(s32[2]{0:T(128)} %pad_add_fusion.place, s32[512]{0:T(512)} %reshape.34.adj, bf16[8,4,3,128,128]{4,3,2,1,0:T(8,128)(2,1)} %bitcast.33, bf16[8,2,2,3,128,128]{5,4,3,2,1,0:T(8,128)(2,1)} %bitcast.36), custom_call_target="tpu_custom_call" | custom-call | tf_op jit(solution)/shard_map/couple/pallas_call | solution.py:273
  138.1 5.5 %all-to-all-start = ((bf16[16,2,128,128]{3,2,1,0:T(8,128)(2,1)}), bf16[16,2,128,128]{3,2,1,0:T(8,128)(2,1)S(1)}, u32[]{:S(2)}, u32[]{:S(2)}) async-start(bf16[16,2,128,128]{3,2,1,0:T(8,128)(2,1)} %couple.1), calls=%async_computation | async-start | bytes 2097152 | tf_op jit(solution)/shard_map/all_to_all | solution.py:280
  145.0 7.4 %assemble.1.front = f32[8,1024,128]{2,1,0:T(8,128)} custom-call(s32[2]{0:T(128)} %pad_add_fusion.place, f32[8,1024,128]{2,1,0:T(8,128)} %bitcast.35, bf16[8,4,3,128,128]{4,3,2,1,0:T(8,128)(2,1)} %bitcast.34), custom_call_target="tpu_custom_call" | custom-call | tf_op jit(solution)/shard_map/assemble/pallas_call | solution.py:282
  152.9 1.2 select_reduce_fusion
  154.1 1.4 fusion.partner
  155.5 6.2 %row_side.1 = (bf16[1024,512]{1,0:T(8,128)(2,1)}, bf16[1024,512]{1,0:T(8,128)(2,1)}, bf16[512,512]{1,0:T(8,128)(2,1)}) custom-call(s32[2]{0:T(128)} %pad_add_fusion.place, s32[256]{0:T(256)} %bitcast.48, bf16[8,6,128,128]{3,2,1,0:T(8,128)(2,1)} %copy-done, bf16[8,6,128,128]{3,2,1,0:T(8,128)(2,1)} %collective-permute-done.4.row_other, ...), custom_call_target="tpu_custom_call" | custom-call | tf_op jit(solution)/shard_map/row_side/pallas_call | solution.py:296
  161.7 1.0 copy-done.1
  162.6 10.2 %update.1 = f32[8,1024,128]{2,1,0:T(8,128)} custom-call(s32[2]{0:T(128)} %pad_add_fusion.place, s32[512]{0:T(512)} %reshape.34.adj, s32[256]{0:T(256)} %bitcast.49, f32[8,1024,128]{2,1,0:T(8,128)} %assemble.1.front, bf16[16,2,128,128]{3,2,1,0:T(8,128)(2,1)} %copy-done.1, bf16[1024,512]{1,0:T(8,128)(2,1)} %get-tuple-element.12.w0r, ...), custom_call_target="tpu_custom_call" | custom-call | tf_op jit(solution)/shard_map/update/pallas_call | solution.py:306
  (45 shorter events, 6.8 us)
Async XLA Ops:
  6.5 126.5 %all-gather.5.cloned.1.call-start = ((), (), s32[]{:S(2)}) async-start(), calls=%async_computation.4 | async-start | bytes 3538944 | tf_op jit(solution)/shard_map/all_gather | solution.py:238
  7.5 8.2 %collective-permute-start = (bf16[2,3,128,128]{3,2,1,0:T(8,128)(2,1)S(1)}, bf16[2,3,128,128]{3,2,1,0:T(8,128)(2,1)S(1)}, u32[]{:S(2)}, u32[]{:S(2)}) collective-permute-start(bf16[2,3,128,128]{3,2,1,0:T(8,128)(2,1)S(1)} %constant_dynamic-slice_fusion), channel_id=1, source_target_pairs={{0,16},{16,0},{32,48},{48,32},{64,80},{80,64},{96,112},{112,96},{1... | collective-permute-start | bytes 589832 | tf_op jit(solution)/shard_map/ppermute | solution.py:237
  16.5 31.5 %copy-start.7 = (s32[128,4]{0,1:T(4,128)S(1)}, s32[128,4]{0,1:T(4,128)}, u32[]{:S(2)}) copy-start(s32[128,4]{0,1:T(4,128)} %param.10) | copy-start | bytes 6148
  17.7 10.0 %collective-permute-start.3 = (bf16[96,128]{1,0:T(8,128)(2,1)S(1)}, bf16[96,128]{1,0:T(8,128)(2,1)S(1)}, u32[]{:S(2)}, u32[]{:S(2)}) collective-permute-start(bf16[96,128]{1,0:T(8,128)(2,1)S(1)} %dynamic-slice_bitcast_fusion), channel_id=1, source_target_pairs={{0,8},{1,24},{2,40},{3,56},{4,72},{5,88},{6,104},{7,120},{8,136},{... | collective-permute-start | bytes 73736 | tf_op jit(solution)/shard_map/ppermute | solution.py:243
  23.8 9.1 %collective-permute-start.2 = (bf16[96,128]{1,0:T(8,128)(2,1)S(1)}, bf16[96,128]{1,0:T(8,128)(2,1)S(1)}, u32[]{:S(2)}, u32[]{:S(2)}) collective-permute-start(bf16[96,128]{1,0:T(8,128)(2,1)S(1)} %dynamic-slice_bitcast_fusion), channel_id=1, source_target_pairs={{0,0},{1,16},{2,32},{3,48},{4,64},{5,80},{6,96},{7,112},{8,128},{9... | collective-permute-start | bytes 73736 | tf_op jit(solution)/shard_map/ppermute | solution.py:242
  33.8 30.7 %all-to-all-start.1 = ((bf16[16,96,128]{2,1,0:T(8,128)(2,1)}), bf16[16,96,128]{2,1,0:T(8,128)(2,1)S(1)}, u32[]{:S(2)}, u32[]{:S(2)}) async-start(bf16[16,96,128]{2,1,0:T(8,128)(2,1)} %broadcast_in_dim.65), calls=%async_computation.1 | async-start | bytes 786432 | tf_op jit(solution)/shard_map/all_to_all | solution.py:245
  43.7 118.0 %all-gather.7.cloned.1.call-start = ((), (), s32[]{:S(2)}) async-start(), calls=%async_computation.5 | async-start | bytes 2359296 | tf_op jit(solution)/shard_map/all_gather | solution.py:261
  45.7 7.5 %collective-permute-start.1 = (f32[5,128,128]{2,1,0:T(8,128)S(1)}, f32[5,128,128]{2,1,0:T(8,128)S(1)}, u32[]{:S(2)}, u32[]{:S(2)}) collective-permute-start(f32[5,128,128]{2,1,0:T(8,128)S(1)} %pad_maximum_fusion), channel_id=1, source_target_pairs={{0,8},{1,9},{2,10},{3,11},{4,12},{5,13},{6,14},{7,15},{16,24},{17,... | collective-permute-start | bytes 983048 | tf_op jit(solution)/shard_map/ppermute | solution.py:248
  64.5 0.7 copy-start.2
  68.0 13.5 %collective-permute-start.5 = (bf16[4,128,128]{2,1,0:T(8,128)(2,1)}, bf16[4,128,128]{2,1,0:T(8,128)(2,1)S(1)}, u32[]{:S(2)}, u32[]{:S(2)}) collective-permute-start(bf16[4,128,128]{2,1,0:T(8,128)(2,1)} %get-tuple-element.10), channel_id=1, source_target_pairs={{0,0},{1,16},{2,32},{3,48},{4,64},{5,80},{6,96},{7,112},{8,128},{9... | collective-permute-start | bytes 393224 | tf_op jit(solution)/shard_map/ppermute | solution.py:258
  81.5 7.5 %collective-permute-start.6 = (bf16[4,128,128]{2,1,0:T(8,128)(2,1)S(1)}, bf16[4,128,128]{2,1,0:T(8,128)(2,1)S(1)}, u32[]{:S(2)}, u32[]{:S(2)}) collective-permute-start(bf16[4,128,128]{2,1,0:T(8,128)(2,1)S(1)} %collective-permute-done.5), channel_id=1, source_target_pairs={{0,16},{16,0},{32,48},{48,32},{64,80},{80,64},{96,112},{112,96},{1... | collective-permute-start | bytes 393224 | tf_op jit(solution)/shard_map/ppermute | solution.py:259
  133.0 5.0 %copy-start = (bf16[8,6,128,128]{3,2,1,0:T(8,128)(2,1)}, bf16[8,6,128,128]{3,2,1,0:T(8,128)(2,1)S(1)}, u32[]{:S(2)}) copy-start(bf16[8,6,128,128]{3,2,1,0:T(8,128)(2,1)S(1)} %all_to_all.21.row_own) | copy-start | bytes 4718596
  133.0 22.4 %collective-permute-start.4 = (bf16[8,6,128,128]{3,2,1,0:T(8,128)(2,1)S(1)}, bf16[8,6,128,128]{3,2,1,0:T(8,128)(2,1)}, u32[]{:S(2)}, u32[]{:S(2)}) collective-permute-start(bf16[8,6,128,128]{3,2,1,0:T(8,128)(2,1)S(1)} %all_to_all.21.row_own), channel_id=1, source_target_pairs={{0,1},{1,0},{2,3},{3,2},{4,5},{5,4},{6,7},{7,6},{8,9},{9,8},{10,11... | collective-permute-start | bytes 4718600 | tf_op jit(solution)/shard_map/ppermute | solution.py:269
  138.1 5.5 %copy-start.4 = (f32[2,512]{1,0:T(2,128)S(1)}, f32[2,512]{1,0:T(2,128)}, u32[]{:S(2)}) copy-start(f32[2,512]{1,0:T(2,128)} %param.14) | copy-start | bytes 12292
  138.1 5.5 %copy-start.5 = (s32[2,512]{1,0:T(2,128)S(1)}, s32[2,512]{1,0:T(2,128)}, u32[]{:S(2)}) copy-start(s32[2,512]{1,0:T(2,128)} %param.12) | copy-start | bytes 12292
  138.1 6.2 %copy-start.3 = (s32[2,512]{1,0:T(2,128)S(1)}, s32[2,512]{1,0:T(2,128)}, u32[]{:S(2)}) copy-start(s32[2,512]{1,0:T(2,128)} %param.11) | copy-start | bytes 12292
  138.1 23.6 %all-to-all-start = ((bf16[16,2,128,128]{3,2,1,0:T(8,128)(2,1)}), bf16[16,2,128,128]{3,2,1,0:T(8,128)(2,1)S(1)}, u32[]{:S(2)}, u32[]{:S(2)}) async-start(bf16[16,2,128,128]{3,2,1,0:T(8,128)(2,1)} %couple.1), calls=%async_computation | async-start | bytes 2097152 | tf_op jit(solution)/shard_map/all_to_all | solution.py:280
  145.0 7.8 %copy-start.6 = (f32[2,512]{1,0:T(2,128)S(1)}, f32[2,512]{1,0:T(2,128)}, u32[]{:S(2)}) copy-start(f32[2,512]{1,0:T(2,128)} %param.13) | copy-start | bytes 12292
  161.6 1.0 copy-start.1
Sparse Core Ops, SparseCore 0:
  16.6 57.3 all-gather.4
  89.9 39.8 all-gather.6

commit v5 on v4

--- a/solution.py
+++ b/solution.py
@@ -262,9 +262,14 @@
 
     cross_row = lax.all_to_all(jnp.broadcast_to(first, (N, NB // 2, NB)), "row", 0, 0, tiled=True)[4:8]
 
-    half = jnp.concatenate([half, cross_row.reshape(2, NB, NB)])
+    cross_row = cross_row.reshape(1, 2, NB, NB)
     row_own = lax.all_to_all(
-        jnp.broadcast_to(half[None], (8,) + half.shape), "col", 0, 0, tiled=True, axis_index_groups=SAME_CORE
+        jnp.concatenate([jnp.broadcast_to(half[None], (8, 4, NB, NB)), jnp.broadcast_to(cross_row, (8, 2, NB, NB))], 1),
+        "col",
+        0,
+        0,
+        tiled=True,
+        axis_index_groups=SAME_CORE,
     )
     row_other = lax.ppermute(row_own, "col", SWAP_CORE)
 

time: 181 us -> 181 us (level)
  transfers between devices with their start and end apart: 11 -> 11, of which waited for: 6 -> 6; matrix products, arithmetic and copies ran while one was open for 8% -> 7% of each run, Pallas kernels for 12% -> 12%
where the time goes in v5:
time: 181 us; the launch traced here: 180 us
  blocking collectives  42 us (23%)
  waiting for transfers between devices  39.4 us (22%)
  starting transfers between devices  36 us (20%)
  Pallas kernels  31.5 us (17%)
  between operations  13.7 us (8%)
  local copies, waits for them, and re-layouts  10.7 us (6%)
  other arithmetic  6.14 us (3%)
    all_to_all x1, blocking collectives, steps(): lax.all_to_all(jnp.concatenate([jnp.broadcast_to(half[None], (8, 4, NB, N...  22.5 us
    all_to_all x1, blocking collectives, steps(): lax.all_to_all(jnp.broadcast_to(first, (N, NB // 2, NB)), 'row', 0, 0, ti...  19.5 us
    ppermute x1, waiting for transfers between devices, steps(): spread = lax.ppermute(half, BOTH, SPREAD)  10.9 us
    all_to_all x1, waiting for transfers between devices, steps(): lax.all_to_all(jnp.broadcast_to(low[None], (N, 96, NB)), 'row', 0, 0, til...  10.5 us
    pallas_call x1, Pallas kernels, steps(): pl.pallas_call(update_kernel, grid=(2,), out_shape=jax.ShapeDtypeStruct((...  10.2 us
    all_to_all x1, starting transfers between devices, steps(): lax.all_to_all(jnp.broadcast_to(low[None], (N, 96, NB)), 'row', 0, 0, til...  9.88 us
    pallas_call x1, Pallas kernels, steps(): pl.pallas_call(assemble_kernel, grid=(8,), out_shape=jax.ShapeDtypeStruct...  7.32 us
    ppermute x1, starting transfers between devices, steps(): low_b = lax.ppermute(low, BOTH, LOW_B)  6.19 us
  transfers between devices with their start and end apart: 11, of which 6 were waited for; matrix products, arithmetic and copies ran while one was open for 7% of the time, Pallas kernels for 12%

profile of v5, /device:TPU:8, one launch (start us, length us, event | category | flops | bytes accessed | tf_op | source)
XLA Modules:
  0.0 179.5 jit_solution(15737452040572590864)
XLA Ops:
  6.5 0.9 constant_dynamic-slice_fusion
  7.5 3.1 %collective-permute-start = (bf16[2,3,128,128]{3,2,1,0:T(8,128)(2,1)S(1)}, bf16[2,3,128,128]{3,2,1,0:T(8,128)(2,1)S(1)}, u32[]{:S(2)}, u32[]{:S(2)}) collective-permute-start(bf16[2,3,128,128]{3,2,1,0:T(8,128)(2,1)S(1)} %constant_dynamic-slice_fusion), channel_id=1, source_target_pairs={{0,16},{16,0},{32,48},{48,32},{64,80},{80,64},{96,112},{112,96},{1... | collective-permute-start | bytes 589832 | tf_op jit(solution)/shard_map/ppermute | solution.py:237
  10.6 0.9 fusion.3
  11.5 4.2 %collective-permute-done = bf16[2,3,128,128]{3,2,1,0:T(8,128)(2,1)S(1)} collective-permute-done((bf16[2,3,128,128]{3,2,1,0:T(8,128)(2,1)S(1)}, bf16[2,3,128,128]{3,2,1,0:T(8,128)(2,1)S(1)}, u32[]{:S(2)}, u32[]{:S(2)}) %collective-permute-start) | collective-permute-done | bytes 196640 | tf_op jit(solution)/shard_map/ppermute | solution.py:237
  15.7 0.8 pad_maximum_fusion.3
  16.6 1.0 slice.39
  17.7 6.2 %collective-permute-start.3 = (bf16[96,128]{1,0:T(8,128)(2,1)S(1)}, bf16[96,128]{1,0:T(8,128)(2,1)S(1)}, u32[]{:S(2)}, u32[]{:S(2)}) collective-permute-start(bf16[96,128]{1,0:T(8,128)(2,1)S(1)} %dynamic-slice_bitcast_fusion), channel_id=1, source_target_pairs={{0,8},{1,24},{2,40},{3,56},{4,72},{5,88},{6,104},{7,120},{8,136},{... | collective-permute-start | bytes 73736 | tf_op jit(solution)/shard_map/ppermute | solution.py:243
  23.9 3.8 %collective-permute-start.2 = (bf16[96,128]{1,0:T(8,128)(2,1)S(1)}, bf16[96,128]{1,0:T(8,128)(2,1)S(1)}, u32[]{:S(2)}, u32[]{:S(2)}) collective-permute-start(bf16[96,128]{1,0:T(8,128)(2,1)S(1)} %dynamic-slice_bitcast_fusion), channel_id=1, source_target_pairs={{0,0},{1,16},{2,32},{3,48},{4,64},{5,80},{6,96},{7,112},{8,128},{9... | collective-permute-start | bytes 73736 | tf_op jit(solution)/shard_map/ppermute | solution.py:242
  27.7 5.3 %collective-permute-done.2 = bf16[96,128]{1,0:T(8,128)(2,1)S(1)} collective-permute-done((bf16[96,128]{1,0:T(8,128)(2,1)S(1)}, bf16[96,128]{1,0:T(8,128)(2,1)S(1)}, u32[]{:S(2)}, u32[]{:S(2)}) %collective-permute-start.2) | collective-permute-done | bytes 24608 | tf_op jit(solution)/shard_map/ppermute | solution.py:242
  33.0 0.8 broadcast_in_dim.72
  33.8 9.9 %all-to-all-start.1 = ((bf16[16,96,128]{2,1,0:T(8,128)(2,1)}), bf16[16,96,128]{2,1,0:T(8,128)(2,1)S(1)}, u32[]{:S(2)}, u32[]{:S(2)}) async-start(bf16[16,96,128]{2,1,0:T(8,128)(2,1)} %broadcast_in_dim.72), calls=%async_computation.1 | async-start | bytes 786432 | tf_op jit(solution)/shard_map/all_to_all | solution.py:245
  43.7 1.1 fusion.2
  44.8 0.8 slice.35
  45.7 2.3 %collective-permute-start.1 = (f32[5,128,128]{2,1,0:T(8,128)S(1)}, f32[5,128,128]{2,1,0:T(8,128)S(1)}, u32[]{:S(2)}, u32[]{:S(2)}) collective-permute-start(f32[5,128,128]{2,1,0:T(8,128)S(1)} %pad_maximum_fusion.1), channel_id=1, source_target_pairs={{0,8},{1,9},{2,10},{3,11},{4,12},{5,13},{6,14},{7,15},{16,24},{17,... | collective-permute-start | bytes 983048 | tf_op jit(solution)/shard_map/ppermute | solution.py:248
  49.5 3.7 %collective-permute-done.1 = f32[5,128,128]{2,1,0:T(8,128)S(1)} collective-permute-done((f32[5,128,128]{2,1,0:T(8,128)S(1)}, f32[5,128,128]{2,1,0:T(8,128)S(1)}, u32[]{:S(2)}, u32[]{:S(2)}) %collective-permute-start.1) | collective-permute-done | bytes 327712 | tf_op jit(solution)/shard_map/ppermute | solution.py:248
  53.2 0.8 fusion.1.base
  54.0 10.5 %all-to-all-done.1.faces = bf16[16,96,128]{2,1,0:T(8,128)(2,1)S(1)} async-done(((bf16[16,96,128]{2,1,0:T(8,128)(2,1)}), bf16[16,96,128]{2,1,0:T(8,128)(2,1)S(1)}, u32[]{:S(2)}, u32[]{:S(2)}) %all-to-all-start.1) | async-done | bytes 393248 | tf_op jit(solution)/shard_map/all_to_all | solution.py:245
  65.2 2.8 %panel_block.1 = (bf16[4,128,128]{2,1,0:T(8,128)(2,1)}, bf16[1,64,128]{2,1,0:T(8,128)(2,1)}) custom-call(s32[2]{0:T(128)} %pad_add_fusion.place, s32[512]{0:T(512)} %reshape.33.adj, f32[5,128,128]{2,1,0:T(8,128)} %fusion.1.base, bf16[8,4,3,128,128]{4,3,2,1,0:T(8,128)(2,1)} %bitcast.32, bf16[16,96,128]{2,1,0:T(8,128)(2,1)} %copy-done.2), custom_call_target="tpu_custom_call" | custom-call | tf_op jit(solution)/shard_map/panel_block/pallas_call | solution.py:249
  68.0 2.7 %collective-permute-start.5 = (bf16[4,128,128]{2,1,0:T(8,128)(2,1)}, bf16[4,128,128]{2,1,0:T(8,128)(2,1)S(1)}, u32[]{:S(2)}, u32[]{:S(2)}) collective-permute-start(bf16[4,128,128]{2,1,0:T(8,128)(2,1)} %get-tuple-element.10), channel_id=1, source_target_pairs={{0,0},{1,16},{2,32},{3,48},{4,64},{5,80},{6,96},{7,112},{8,128},{9... | collective-permute-start | bytes 393224 | tf_op jit(solution)/shard_map/ppermute | solution.py:258
  70.7 10.9 %collective-permute-done.5 = bf16[4,128,128]{2,1,0:T(8,128)(2,1)S(1)} collective-permute-done((bf16[4,128,128]{2,1,0:T(8,128)(2,1)}, bf16[4,128,128]{2,1,0:T(8,128)(2,1)S(1)}, u32[]{:S(2)}, u32[]{:S(2)}) %collective-permute-start.5) | collective-permute-done | bytes 131104 | tf_op jit(solution)/shard_map/ppermute | solution.py:258
  81.6 2.6 %collective-permute-start.6 = (bf16[4,128,128]{2,1,0:T(8,128)(2,1)S(1)}, bf16[4,128,128]{2,1,0:T(8,128)(2,1)S(1)}, u32[]{:S(2)}, u32[]{:S(2)}) collective-permute-start(bf16[4,128,128]{2,1,0:T(8,128)(2,1)S(1)} %collective-permute-done.5), channel_id=1, source_target_pairs={{0,16},{16,0},{32,48},{48,32},{64,80},{80,64},{96,112},{112,96},{1... | collective-permute-start | bytes 393224 | tf_op jit(solution)/shard_map/ppermute | solution.py:259
  84.3 4.8 %collective-permute-done.6 = bf16[4,128,128]{2,1,0:T(8,128)(2,1)S(1)} collective-permute-done((bf16[4,128,128]{2,1,0:T(8,128)(2,1)S(1)}, bf16[4,128,128]{2,1,0:T(8,128)(2,1)S(1)}, u32[]{:S(2)}, u32[]{:S(2)}) %collective-permute-start.6) | collective-permute-done | bytes 131104 | tf_op jit(solution)/shard_map/ppermute | solution.py:259
  90.5 19.5 %all_to_all.20 = bf16[16,64,128]{2,1,0:T(8,128)(2,1)S(1)} all-to-all(bf16[16,64,128]{2,1,0:T(8,128)(2,1)S(1)} %broadcast_in_dim.75), channel_id=1, replica_groups=mesh['row'=16,'col'=16] {'row'}, dimensions={0} | all-to-all | bytes 524288 | tf_op jit(solution)/shard_map/all_to_all | solution.py:263
  110.6 22.5 %all_to_all.21.row_own = bf16[8,6,128,128]{3,2,1,0:T(8,128)(2,1)S(1)} all-to-all(bf16[8,6,128,128]{3,2,1,0:T(8,128)(2,1)S(1)} %pad_maximum_fusion), channel_id=1, replica_groups={{0,2,4,6,8,10,12,14},{1,3,5,7,9,11,13,15},{16,18,20,22,24,26,28,30},{17..., dimensions={0} | all-to-all | bytes 3145728 | tf_op jit(solution)/shard_map/all_to_all | solution.py:266
  133.1 5.0 %couple.1 = bf16[16,2,128,128]{3,2,1,0:T(8,128)(2,1)} custom-call(s32[2]{0:T(128)} %pad_add_fusion.place, s32[512]{0:T(512)} %reshape.33.adj, bf16[8,4,3,128,128]{4,3,2,1,0:T(8,128)(2,1)} %bitcast.33, bf16[8,2,2,3,128,128]{5,4,3,2,1,0:T(8,128)(2,1)} %bitcast.36), custom_call_target="tpu_custom_call" | custom-call | tf_op jit(solution)/shard_map/couple/pallas_call | solution.py:278
  138.1 5.4 %all-to-all-start = ((bf16[16,2,128,128]{3,2,1,0:T(8,128)(2,1)}), bf16[16,2,128,128]{3,2,1,0:T(8,128)(2,1)S(1)}, u32[]{:S(2)}, u32[]{:S(2)}) async-start(bf16[16,2,128,128]{3,2,1,0:T(8,128)(2,1)} %couple.1), calls=%async_computation | async-start | bytes 2097152 | tf_op jit(solution)/shard_map/all_to_all | solution.py:285
  145.0 7.3 %assemble.1.front = f32[8,1024,128]{2,1,0:T(8,128)} custom-call(s32[2]{0:T(128)} %pad_add_fusion.place, f32[8,1024,128]{2,1,0:T(8,128)} %bitcast.35, bf16[8,4,3,128,128]{4,3,2,1,0:T(8,128)(2,1)} %bitcast.34), custom_call_target="tpu_custom_call" | custom-call | tf_op jit(solution)/shard_map/assemble/pallas_call | solution.py:287
  152.8 1.2 select_reduce_fusion
  153.9 1.4 fusion.partner
  155.3 6.2 %row_side.1 = (bf16[1024,512]{1,0:T(8,128)(2,1)}, bf16[1024,512]{1,0:T(8,128)(2,1)}, bf16[512,512]{1,0:T(8,128)(2,1)}) custom-call(s32[2]{0:T(128)} %pad_add_fusion.place, s32[256]{0:T(256)} %bitcast.48, bf16[8,6,128,128]{3,2,1,0:T(8,128)(2,1)} %copy-done, bf16[8,6,128,128]{3,2,1,0:T(8,128)(2,1)} %collective-permute-done.4.row_other, ...), custom_call_target="tpu_custom_call" | custom-call | tf_op jit(solution)/shard_map/row_side/pallas_call | solution.py:301
  161.5 1.0 copy-done.1
  162.5 10.2 %update.1 = f32[8,1024,128]{2,1,0:T(8,128)} custom-call(s32[2]{0:T(128)} %pad_add_fusion.place, s32[512]{0:T(512)} %reshape.33.adj, s32[256]{0:T(256)} %bitcast.49, f32[8,1024,128]{2,1,0:T(8,128)} %assemble.1.front, bf16[16,2,128,128]{3,2,1,0:T(8,128)(2,1)} %copy-done.1, bf16[1024,512]{1,0:T(8,128)(2,1)} %get-tuple-element.12.w0r, ...), custom_call_target="tpu_custom_call" | custom-call | tf_op jit(solution)/shard_map/update/pallas_call | solution.py:311
  (48 shorter events, 6.2 us)
Async XLA Ops:
  6.5 126.5 %all-gather.5.cloned.1.call-start = ((), (), s32[]{:S(2)}) async-start(), calls=%async_computation.4 | async-start | bytes 3538944 | tf_op jit(solution)/shard_map/all_gather | solution.py:238
  7.5 8.2 %collective-permute-start = (bf16[2,3,128,128]{3,2,1,0:T(8,128)(2,1)S(1)}, bf16[2,3,128,128]{3,2,1,0:T(8,128)(2,1)S(1)}, u32[]{:S(2)}, u32[]{:S(2)}) collective-permute-start(bf16[2,3,128,128]{3,2,1,0:T(8,128)(2,1)S(1)} %constant_dynamic-slice_fusion), channel_id=1, source_target_pairs={{0,16},{16,0},{32,48},{48,32},{64,80},{80,64},{96,112},{112,96},{1... | collective-permute-start | bytes 589832 | tf_op jit(solution)/shard_map/ppermute | solution.py:237
  16.5 31.5 %copy-start.8 = (s32[128,4]{0,1:T(4,128)S(1)}, s32[128,4]{0,1:T(4,128)}, u32[]{:S(2)}) copy-start(s32[128,4]{0,1:T(4,128)} %param.10) | copy-start | bytes 6148
  17.7 10.0 %collective-permute-start.3 = (bf16[96,128]{1,0:T(8,128)(2,1)S(1)}, bf16[96,128]{1,0:T(8,128)(2,1)S(1)}, u32[]{:S(2)}, u32[]{:S(2)}) collective-permute-start(bf16[96,128]{1,0:T(8,128)(2,1)S(1)} %dynamic-slice_bitcast_fusion), channel_id=1, source_target_pairs={{0,8},{1,24},{2,40},{3,56},{4,72},{5,88},{6,104},{7,120},{8,136},{... | collective-permute-start | bytes 73736 | tf_op jit(solution)/shard_map/ppermute | solution.py:243
  23.9 9.1 %collective-permute-start.2 = (bf16[96,128]{1,0:T(8,128)(2,1)S(1)}, bf16[96,128]{1,0:T(8,128)(2,1)S(1)}, u32[]{:S(2)}, u32[]{:S(2)}) collective-permute-start(bf16[96,128]{1,0:T(8,128)(2,1)S(1)} %dynamic-slice_bitcast_fusion), channel_id=1, source_target_pairs={{0,0},{1,16},{2,32},{3,48},{4,64},{5,80},{6,96},{7,112},{8,128},{9... | collective-permute-start | bytes 73736 | tf_op jit(solution)/shard_map/ppermute | solution.py:242
  33.8 30.7 %all-to-all-start.1 = ((bf16[16,96,128]{2,1,0:T(8,128)(2,1)}), bf16[16,96,128]{2,1,0:T(8,128)(2,1)S(1)}, u32[]{:S(2)}, u32[]{:S(2)}) async-start(bf16[16,96,128]{2,1,0:T(8,128)(2,1)} %broadcast_in_dim.72), calls=%async_computation.1 | async-start | bytes 786432 | tf_op jit(solution)/shard_map/all_to_all | solution.py:245
  43.7 117.8 %all-gather.7.cloned.1.call-start = ((), (), s32[]{:S(2)}) async-start(), calls=%async_computation.5 | async-start | bytes 2359296 | tf_op jit(solution)/shard_map/all_gather | solution.py:261
  45.7 7.5 %collective-permute-start.1 = (f32[5,128,128]{2,1,0:T(8,128)S(1)}, f32[5,128,128]{2,1,0:T(8,128)S(1)}, u32[]{:S(2)}, u32[]{:S(2)}) collective-permute-start(f32[5,128,128]{2,1,0:T(8,128)S(1)} %pad_maximum_fusion.1), channel_id=1, source_target_pairs={{0,8},{1,9},{2,10},{3,11},{4,12},{5,13},{6,14},{7,15},{16,24},{17,... | collective-permute-start | bytes 983048 | tf_op jit(solution)/shard_map/ppermute | solution.py:248
  64.5 0.7 copy-start.2
  68.0 42.2 %copy-start.3 = (bf16[4,128,128]{2,1,0:T(8,128)(2,1)S(1)}, bf16[4,128,128]{2,1,0:T(8,128)(2,1)}, u32[]{:S(2)}) copy-start(bf16[4,128,128]{2,1,0:T(8,128)(2,1)} %get-tuple-element.10) | copy-start | bytes 393220
  68.0 13.6 %collective-permute-start.5 = (bf16[4,128,128]{2,1,0:T(8,128)(2,1)}, bf16[4,128,128]{2,1,0:T(8,128)(2,1)S(1)}, u32[]{:S(2)}, u32[]{:S(2)}) collective-permute-start(bf16[4,128,128]{2,1,0:T(8,128)(2,1)} %get-tuple-element.10), channel_id=1, source_target_pairs={{0,0},{1,16},{2,32},{3,48},{4,64},{5,80},{6,96},{7,112},{8,128},{9... | collective-permute-start | bytes 393224 | tf_op jit(solution)/shard_map/ppermute | solution.py:258
  81.6 7.4 %collective-permute-start.6 = (bf16[4,128,128]{2,1,0:T(8,128)(2,1)S(1)}, bf16[4,128,128]{2,1,0:T(8,128)(2,1)S(1)}, u32[]{:S(2)}, u32[]{:S(2)}) collective-permute-start(bf16[4,128,128]{2,1,0:T(8,128)(2,1)S(1)} %collective-permute-done.5), channel_id=1, source_target_pairs={{0,16},{16,0},{32,48},{48,32},{64,80},{80,64},{96,112},{112,96},{1... | collective-permute-start | bytes 393224 | tf_op jit(solution)/shard_map/ppermute | solution.py:259
  133.1 5.0 %copy-start = (bf16[8,6,128,128]{3,2,1,0:T(8,128)(2,1)}, bf16[8,6,128,128]{3,2,1,0:T(8,128)(2,1)S(1)}, u32[]{:S(2)}) copy-start(bf16[8,6,128,128]{3,2,1,0:T(8,128)(2,1)S(1)} %all_to_all.21.row_own) | copy-start | bytes 4718596
  133.1 22.3 %collective-permute-start.4 = (bf16[8,6,128,128]{3,2,1,0:T(8,128)(2,1)S(1)}, bf16[8,6,128,128]{3,2,1,0:T(8,128)(2,1)}, u32[]{:S(2)}, u32[]{:S(2)}) collective-permute-start(bf16[8,6,128,128]{3,2,1,0:T(8,128)(2,1)S(1)} %all_to_all.21.row_own), channel_id=1, source_target_pairs={{0,1},{1,0},{2,3},{3,2},{4,5},{5,4},{6,7},{7,6},{8,9},{9,8},{10,11... | collective-permute-start | bytes 4718600 | tf_op jit(solution)/shard_map/ppermute | solution.py:274
  138.1 5.4 %copy-start.5 = (f32[2,512]{1,0:T(2,128)S(1)}, f32[2,512]{1,0:T(2,128)}, u32[]{:S(2)}) copy-start(f32[2,512]{1,0:T(2,128)} %param.14) | copy-start | bytes 12292
  138.1 5.4 %copy-start.6 = (s32[2,512]{1,0:T(2,128)S(1)}, s32[2,512]{1,0:T(2,128)}, u32[]{:S(2)}) copy-start(s32[2,512]{1,0:T(2,128)} %param.12) | copy-start | bytes 12292
  138.1 6.1 %copy-start.4 = (s32[2,512]{1,0:T(2,128)S(1)}, s32[2,512]{1,0:T(2,128)}, u32[]{:S(2)}) copy-start(s32[2,512]{1,0:T(2,128)} %param.11) | copy-start | bytes 12292
  138.1 23.4 %all-to-all-start = ((bf16[16,2,128,128]{3,2,1,0:T(8,128)(2,1)}), bf16[16,2,128,128]{3,2,1,0:T(8,128)(2,1)S(1)}, u32[]{:S(2)}, u32[]{:S(2)}) async-start(bf16[16,2,128,128]{3,2,1,0:T(8,128)(2,1)} %couple.1), calls=%async_computation | async-start | bytes 2097152 | tf_op jit(solution)/shard_map/all_to_all | solution.py:285
  145.0 7.8 %copy-start.7 = (f32[2,512]{1,0:T(2,128)S(1)}, f32[2,512]{1,0:T(2,128)}, u32[]{:S(2)}) copy-start(f32[2,512]{1,0:T(2,128)} %param.13) | copy-start | bytes 12292
  161.5 1.0 copy-start.1
Sparse Core Ops, SparseCore 0:
  16.7 57.1 all-gather.4
  89.9 39.7 all-gather.6
